TPU v7x, 512 devices: a whole 4x8x8 slice. The times are simulated.
512 devices in a mesh: pipe: 16 (over y, core), expert: 32 (over x, z).
Axes of the slice: x: 4, y: 8, z: 8, core: 2. Of those that a mesh axis runs over, the one named last changes fastest.
Arguments:
- fwd_state: bfloat16 [16, 2048, 2048], P('pipe', 'expert'), may hold values from -6 to 6
- rev_state: bfloat16 [16, 2048, 2048], P('pipe', 'expert'), may hold values from -6 to 6
- norm_gain: float32 [16, 2048], P('pipe'), may hold values from 0.1 to 1.9
- gate_weight: bfloat16 [16, 2048, 6144], P('pipe', None, 'expert'), may hold values from -0.125 to 0.125
- up_weight: bfloat16 [16, 2048, 6144], P('pipe', None, 'expert'), may hold values from -0.125 to 0.125
- down_weight: bfloat16 [16, 6144, 2048], P('pipe', 'expert'), may hold values from -0.21875 to 0.21875
- fwd_routes: int32 [2, 16, 2048, 2], P(None, 'pipe', 'expert'), may hold values from 0 to 7, all different within a row; in each aligned block of 64 rows (0 to 63, 64 to 127, ..., all dimensions but the last counted through in order) at most 24 rows name the same one
- rev_routes: int32 [2, 16, 2048, 2], P(None, 'pipe', 'expert'), may hold values from 0 to 7, all different within a row; in each aligned block of 64 rows (0 to 63, 64 to 127, ..., all dimensions but the last counted through in order) at most 24 rows name the same one
- fwd_combine: float32 [2, 16, 2048, 2], P(None, 'pipe', 'expert'), may hold values from 0.2 to 1
- rev_combine: float32 [2, 16, 2048, 2], P(None, 'pipe', 'expert'), may hold values from 0.2 to 1
Outputs:
- fwd_out: bfloat16 [16, 2048, 2048], P('pipe', 'expert')
- rev_out: bfloat16 [16, 2048, 2048], P('pipe', 'expert')
Inputs may be any that keep to these rules, and one draw needn't show every extreme that they name: `fwd_routes`: each token's 2 ids are distinct. In each aligned block of 64 tokens (one device's tokens for one application and section) no expert is chosen by more than 24 tokens, a bound that some block reaches; every expert is chosen somewhere. `rev_routes`: as for fwd_routes.
All inputs are finite; a program needn't handle non-finite values.
Results may differ from a plain program's by a relative error of at most 0.0068.
Values may be sent and summed in bfloat16 or wider, within the bound.
A program may use at most 128 MiB of HBM per device.

v0:
```python
import jax
import jax.numpy as jnp
from jax import lax
from jax.sharding import PartitionSpec as P

EXPERTS = 8
TOPK = 2
TICKS = 2
CAP = 24


def from_behind(block, axis, distance):
    devices = range(lax.axis_size(axis))
    route = [((i - distance) % len(devices), i) for i in devices]
    return lax.ppermute(block, axis, route)


def expert_rows(received, gate_local, up_local, down_local):
    width = received.shape[-1]
    token_rows = received.reshape(-1, width)
    gate_act = jnp.dot(token_rows, gate_local, preferred_element_type=jnp.float32)
    up_act = jnp.dot(token_rows, up_local, preferred_element_type=jnp.float32)
    activated = (jax.nn.silu(gate_act) * up_act).astype(jnp.bfloat16)
    partial_value = jnp.dot(activated, down_local, preferred_element_type=jnp.float32).astype(
        jnp.bfloat16
    )
    return partial_value.reshape(received.shape)


def send_back(partial_value):
    return lax.all_to_all(partial_value, "expert", split_axis=0, concat_axis=0, tiled=True)


def section_layer(
    hidden, route_ids, route_weights, gain_row, gate_local, up_local, down_local, group_size
):
    tok_count = hidden.shape[0]
    width = hidden.shape[1]
    member_count = group_size * EXPERTS
    widened = hidden.astype(jnp.float32)
    scale_inv = lax.rsqrt(jnp.mean(widened * widened, axis=-1, keepdims=True) + 1e-06)
    normed = (widened * scale_inv * gain_row).astype(jnp.bfloat16)
    flat_ids = route_ids.reshape(-1)
    expert_hot = (flat_ids[:, None] == jnp.arange(EXPERTS, dtype=jnp.int32)[None, :]).astype(
        jnp.int32
    )
    before = jnp.cumsum(expert_hot, axis=0) - expert_hot
    slot_rank = jnp.sum(before * expert_hot, axis=1)
    position = flat_ids * CAP + slot_rank
    slot_hot = position[:, None] == jnp.arange(EXPERTS * CAP, dtype=jnp.int32)[None, :]
    slot_hot = slot_hot.reshape(tok_count, TOPK, EXPERTS * CAP)
    send_rows = jnp.einsum(
        "tke,td->ed", slot_hot.astype(jnp.bfloat16), normed, preferred_element_type=jnp.float32
    ).astype(jnp.bfloat16)
    combine_mat = jnp.sum(slot_hot.astype(jnp.float32) * route_weights[:, :, None], axis=1)
    copies = jnp.broadcast_to(
        send_rows.reshape(EXPERTS, 1, CAP, width), (EXPERTS, group_size, CAP, width)
    ).reshape(member_count, CAP, width)
    partial_value = expert_rows(
        lax.all_to_all(copies, "expert", split_axis=0, concat_axis=0, tiled=True),
        gate_local,
        up_local,
        down_local,
    )
    returned = send_back(partial_value)
    summed = jnp.sum(returned.reshape(EXPERTS, group_size, CAP, width).astype(jnp.float32), axis=1)
    summed = summed.reshape(EXPERTS * CAP, width)
    expert_out = jnp.dot(combine_mat, summed, precision=lax.Precision.HIGHEST)
    return (widened + expert_out).astype(jnp.bfloat16)


def body(
    fwd_state,
    rev_state,
    norm_gain,
    gate_weight,
    up_weight,
    down_weight,
    fwd_routes,
    rev_routes,
    fwd_combine,
    rev_combine,
):
    member_count = lax.axis_size("expert")
    group_size = member_count // EXPERTS
    gain_row = norm_gain[0]
    gate_local = gate_weight[0]
    up_local = up_weight[0]
    down_local = down_weight[0]
    fwd_now = fwd_state[0]
    rev_now = rev_state[0]
    for tick_index in range(TICKS):
        fwd_next = section_layer(
            fwd_now,
            fwd_routes[tick_index, 0],
            fwd_combine[tick_index, 0],
            gain_row,
            gate_local,
            up_local,
            down_local,
            group_size,
        )
        rev_next = section_layer(
            rev_now,
            rev_routes[tick_index, 0],
            rev_combine[tick_index, 0],
            gain_row,
            gate_local,
            up_local,
            down_local,
            group_size,
        )
        if tick_index + 1 < TICKS:
            fwd_now = from_behind(fwd_next, "pipe", 1)
            rev_now = from_behind(rev_next, "pipe", -1)
    return (fwd_next[None], rev_next[None])


def solution(mesh):
    placed = (
        P("pipe", "expert", None),
        P("pipe", "expert", None),
        P("pipe", None),
        P("pipe", None, "expert"),
        P("pipe", None, "expert"),
        P("pipe", "expert", None),
        P(None, "pipe", "expert", None),
        P(None, "pipe", "expert", None),
        P(None, "pipe", "expert", None),
        P(None, "pipe", "expert", None),
    )
    return jax.shard_map(
        body,
        mesh=mesh,
        in_specs=placed,
        out_specs=(P("pipe", "expert", None), P("pipe", "expert", None)),
        check_vma=False,
    )
```

profile of v0, /device:TPU:32, one launch (start us, length us, event | category | flops | bytes accessed | tf_op | source)
XLA Modules:
  0.0 667.5 jit_solution(4779508879883582630)
XLA Ops:
  0.6 0.8 fusion.93
  1.8 0.2 reduce_window_sum.22
  1.9 0.2 select_reduce_fusion.7
  2.1 0.1 reduce_sum.189
  2.4 0.2 eq.123
  2.7 0.2 reduce_window_sum.23
  2.8 0.2 select_reduce_fusion.6
  3.0 0.1 reduce_sum.195
  3.2 0.7 slice_bitcast_fusion.3
  4.0 1.1 fusion.56
  5.1 0.7 bitcast_add_fusion.3
  5.9 1.4 convolution_convert_fusion.7
  7.3 2.1 broadcast_in_dim.21
  9.3 13.4 %all-to-all-start = ((bf16[32,24,2048]{2,1,0:T(8,128)(2,1)}), bf16[32,24,2048]{2,1,0:T(8,128)(2,1)}, u32[]{:S(2)}, u32[]{:S(2)}) async-start(bf16[32,24,2048]{2,1,0:T(8,128)(2,1)} %bitcast.128), calls=%async_computation | async-start | bytes 6291456 | tf_op jit(solution)/shard_map/all_to_all | solution.py:60
  22.9 0.1 eq.130
  23.1 0.2 reduce_window_sum.27
  23.3 0.2 select_reduce_fusion.5
  23.5 0.1 reduce_sum.201
  23.8 0.2 eq.137
  24.0 0.2 reduce_window_sum.32
  24.2 0.2 select_reduce_fusion.4
  24.4 0.1 reduce_sum.207
  24.7 0.2 fusion.59
  24.9 0.4 convolution_convert_fusion.5
  25.4 72.1 %all-to-all-done = bf16[32,24,2048]{2,1,0:T(8,128)(2,1)} async-done(((bf16[32,24,2048]{2,1,0:T(8,128)(2,1)}), bf16[32,24,2048]{2,1,0:T(8,128)(2,1)}, u32[]{:S(2)}, u32[]{:S(2)}) %all-to-all-start) | async-done | bytes 3145760 | tf_op jit(solution)/shard_map/all_to_all | solution.py:60
  97.4 2.0 broadcast_in_dim.26
  99.5 6.1 all-to-all-start.4
  105.6 4.0 fusion.28
  109.6 6.2 convolution_convert_fusion.3
  115.7 64.4 %all-to-all-done.4 = bf16[32,24,2048]{2,1,0:T(8,128)(2,1)} async-done(((bf16[32,24,2048]{2,1,0:T(8,128)(2,1)}), bf16[32,24,2048]{2,1,0:T(8,128)(2,1)}, u32[]{:S(2)}, u32[]{:S(2)}) %all-to-all-start.4) | async-done | bytes 3145760 | tf_op jit(solution)/shard_map/all_to_all | solution.py:60
  180.2 5.9 all-to-all-start.1
  186.0 3.9 fusion.24
  190.0 6.1 convolution_convert_fusion.1
  196.0 64.4 %all-to-all-done.1 = bf16[32,24,2048]{2,1,0:T(8,128)(2,1)} async-done(((bf16[32,24,2048]{2,1,0:T(8,128)(2,1)}), bf16[32,24,2048]{2,1,0:T(8,128)(2,1)}, u32[]{:S(2)}, u32[]{:S(2)}) %all-to-all-start.1) | async-done | bytes 3145760 | tf_op jit(solution)/shard_map/all_to_all | solution.py:31
  260.5 6.0 all-to-all-start.5
  266.5 2.7 convert_reduce_fusion.3
  269.2 1.1 fusion
  270.4 6.9 %collective-permute-done = bf16[64,2048]{1,0:T(8,128)(2,1)S(1)} collective-permute-done((bf16[64,2048]{1,0:T(8,128)(2,1)S(1)}, bf16[64,2048]{1,0:T(8,128)(2,1)S(1)}, u32[]{:S(2)}, u32[]{:S(2)}) %collective-permute-start) | collective-permute-done | bytes 262176 | tf_op jit(solution)/shard_map/ppermute | solution.py:15
  277.3 0.2 fusion.50
  277.5 0.4 convolution_convert_fusion.6
  277.9 62.7 %all-to-all-done.5 = bf16[32,24,2048]{2,1,0:T(8,128)(2,1)} async-done(((bf16[32,24,2048]{2,1,0:T(8,128)(2,1)}), bf16[32,24,2048]{2,1,0:T(8,128)(2,1)}, u32[]{:S(2)}, u32[]{:S(2)}) %all-to-all-start.5) | async-done | bytes 3145760 | tf_op jit(solution)/shard_map/all_to_all | solution.py:31
  340.6 2.1 broadcast_in_dim.23
  342.7 5.3 all-to-all-start.2
  348.0 2.7 convert_reduce_fusion.1
  350.7 1.1 fusion.2
  351.9 3.8 collective-permute-done.1
  355.7 0.2 fusion.53
  355.9 0.4 convolution_convert_fusion.4
  356.3 65.9 %all-to-all-done.2 = bf16[32,24,2048]{2,1,0:T(8,128)(2,1)} async-done(((bf16[32,24,2048]{2,1,0:T(8,128)(2,1)}), bf16[32,24,2048]{2,1,0:T(8,128)(2,1)}, u32[]{:S(2)}, u32[]{:S(2)}) %all-to-all-start.2) | async-done | bytes 3145760 | tf_op jit(solution)/shard_map/all_to_all | solution.py:60
  422.2 2.0 broadcast_in_dim.28
  424.2 5.4 all-to-all-start.6
  429.6 4.0 fusion.26
  433.6 6.2 convolution_convert_fusion.2
  439.8 63.6 %all-to-all-done.6 = bf16[32,24,2048]{2,1,0:T(8,128)(2,1)} async-done(((bf16[32,24,2048]{2,1,0:T(8,128)(2,1)}), bf16[32,24,2048]{2,1,0:T(8,128)(2,1)}, u32[]{:S(2)}, u32[]{:S(2)}) %all-to-all-start.6) | async-done | bytes 3145760 | tf_op jit(solution)/shard_map/all_to_all | solution.py:60
  503.4 4.8 all-to-all-start.3
  508.2 3.9 fusion.22
  512.1 6.1 convolution_convert_fusion
  518.2 64.1 %all-to-all-done.3 = bf16[32,24,2048]{2,1,0:T(8,128)(2,1)} async-done(((bf16[32,24,2048]{2,1,0:T(8,128)(2,1)}), bf16[32,24,2048]{2,1,0:T(8,128)(2,1)}, u32[]{:S(2)}, u32[]{:S(2)}) %all-to-all-start.3) | async-done | bytes 3145760 | tf_op jit(solution)/shard_map/all_to_all | solution.py:31
  582.3 5.1 all-to-all-start.7
  587.4 2.6 convert_reduce_fusion.2
  590.1 71.2 %all-to-all-done.7 = bf16[32,24,2048]{2,1,0:T(8,128)(2,1)} async-done(((bf16[32,24,2048]{2,1,0:T(8,128)(2,1)}), bf16[32,24,2048]{2,1,0:T(8,128)(2,1)}, u32[]{:S(2)}, u32[]{:S(2)}) %all-to-all-start.7) | async-done | bytes 3145760 | tf_op jit(solution)/shard_map/all_to_all | solution.py:31
  661.3 2.7 convert_reduce_fusion
  664.0 1.8 fusion.5
  665.8 1.8 fusion.4
  (46 shorter events, 1.7 us)
Async XLA Ops:
  0.6 108.9 %copy-start = (bf16[1,192,2048]{2,1,0:T(8,128)(2,1)S(1)}, bf16[1,192,2048]{2,1,0:T(8,128)(2,1)}, u32[]{:S(2)}) copy-start(bf16[1,192,2048]{2,1,0:T(8,128)(2,1)} %param.15) | copy-start | bytes 2359300
  9.3 13.4 %copy-start.4 = (s32[2,1,64,2]{2,3,1,0:T(2,128)S(1)}, s32[2,1,64,2]{2,3,1,0:T(2,128)}, u32[]{:S(2)}) copy-start(s32[2,1,64,2]{2,3,1,0:T(2,128)} %param.17) | copy-start | bytes 3076
  9.3 15.3 %copy-start.5 = (f32[2,1,64,2]{2,3,1,0:T(2,128)S(1)}, f32[2,1,64,2]{2,3,1,0:T(2,128)}, u32[]{:S(2)}) copy-start(f32[2,1,64,2]{2,3,1,0:T(2,128)} %param.19) | copy-start | bytes 3076
  9.3 15.4 %copy-start.2 = (bf16[1,64,2048]{2,1,0:T(8,128)(2,1)S(1)}, bf16[1,64,2048]{2,1,0:T(8,128)(2,1)}, u32[]{:S(2)}) copy-start(bf16[1,64,2048]{2,1,0:T(8,128)(2,1)} %param.11) | copy-start | bytes 786436
  9.3 15.6 %copy-start.3 = (f32[1,2048]{1,0:T(1,128)S(1)}, f32[1,2048]{1,0:T(1,128)}, u32[]{:S(2)}) copy-start(f32[1,2048]{1,0:T(1,128)} %param.12) | copy-start | bytes 24580
  9.3 88.1 %all-to-all-start = ((bf16[32,24,2048]{2,1,0:T(8,128)(2,1)}), bf16[32,24,2048]{2,1,0:T(8,128)(2,1)}, u32[]{:S(2)}, u32[]{:S(2)}) async-start(bf16[32,24,2048]{2,1,0:T(8,128)(2,1)} %bitcast.128), calls=%async_computation | async-start | bytes 6291456 | tf_op jit(solution)/shard_map/all_to_all | solution.py:60
  99.4 6.1 copy-start.6
  99.5 80.7 %all-to-all-start.4 = ((bf16[32,24,2048]{2,1,0:T(8,128)(2,1)}), bf16[32,24,2048]{2,1,0:T(8,128)(2,1)}, u32[]{:S(2)}, u32[]{:S(2)}) async-start(bf16[32,24,2048]{2,1,0:T(8,128)(2,1)} %bitcast.130), calls=%async_computation.4 | async-start | bytes 6291456 | tf_op jit(solution)/shard_map/all_to_all | solution.py:60
  105.6 4.0 copy-start.8
  180.2 80.3 %all-to-all-start.1 = ((bf16[32,24,2048]{2,1,0:T(8,128)(2,1)}), bf16[32,24,2048]{2,1,0:T(8,128)(2,1)}, u32[]{:S(2)}, u32[]{:S(2)}) async-start(bf16[32,24,2048]{2,1,0:T(8,128)(2,1)} %bitcast.137), calls=%async_computation.1 | async-start | bytes 6291456 | tf_op jit(solution)/shard_map/all_to_all | solution.py:31
  260.5 80.1 %all-to-all-start.5 = ((bf16[32,24,2048]{2,1,0:T(8,128)(2,1)}), bf16[32,24,2048]{2,1,0:T(8,128)(2,1)}, u32[]{:S(2)}, u32[]{:S(2)}) async-start(bf16[32,24,2048]{2,1,0:T(8,128)(2,1)} %bitcast.136), calls=%async_computation.5 | async-start | bytes 6291456 | tf_op jit(solution)/shard_map/all_to_all | solution.py:31
  266.5 2.7 copy-start.1
  270.3 7.0 %collective-permute-start = (bf16[64,2048]{1,0:T(8,128)(2,1)S(1)}, bf16[64,2048]{1,0:T(8,128)(2,1)S(1)}, u32[]{:S(2)}, u32[]{:S(2)}) collective-permute-start(bf16[64,2048]{1,0:T(8,128)(2,1)S(1)} %fusion), channel_id=1, source_target_pairs={{480,0},{0,32},{32,64},{64,96},{96,128},{128,160},{160,192},{192,2... | collective-permute-start | bytes 786440 | tf_op jit(solution)/shard_map/ppermute | solution.py:15
  342.7 79.5 %all-to-all-start.2 = ((bf16[32,24,2048]{2,1,0:T(8,128)(2,1)}), bf16[32,24,2048]{2,1,0:T(8,128)(2,1)}, u32[]{:S(2)}, u32[]{:S(2)}) async-start(bf16[32,24,2048]{2,1,0:T(8,128)(2,1)} %bitcast.129), calls=%async_computation.2 | async-start | bytes 6291456 | tf_op jit(solution)/shard_map/all_to_all | solution.py:60
  351.8 3.9 collective-permute-start.1
  424.2 5.4 copy-start.7
  424.2 79.2 %all-to-all-start.6 = ((bf16[32,24,2048]{2,1,0:T(8,128)(2,1)}), bf16[32,24,2048]{2,1,0:T(8,128)(2,1)}, u32[]{:S(2)}, u32[]{:S(2)}) async-start(bf16[32,24,2048]{2,1,0:T(8,128)(2,1)} %bitcast.131), calls=%async_computation.6 | async-start | bytes 6291456 | tf_op jit(solution)/shard_map/all_to_all | solution.py:60
  429.6 4.0 copy-start.9
  503.4 78.9 %all-to-all-start.3 = ((bf16[32,24,2048]{2,1,0:T(8,128)(2,1)}), bf16[32,24,2048]{2,1,0:T(8,128)(2,1)}, u32[]{:S(2)}, u32[]{:S(2)}) async-start(bf16[32,24,2048]{2,1,0:T(8,128)(2,1)} %bitcast.138), calls=%async_computation.3 | async-start | bytes 6291456 | tf_op jit(solution)/shard_map/all_to_all | solution.py:31
  582.3 79.0 %all-to-all-start.7 = ((bf16[32,24,2048]{2,1,0:T(8,128)(2,1)}), bf16[32,24,2048]{2,1,0:T(8,128)(2,1)}, u32[]{:S(2)}, u32[]{:S(2)}) async-start(bf16[32,24,2048]{2,1,0:T(8,128)(2,1)} %bitcast.139), calls=%async_computation.7 | async-start | bytes 6291456 | tf_op jit(solution)/shard_map/all_to_all | solution.py:31
where the time goes:
time: 668 us
  waiting for transfers between devices  539 us (81%)
  starting transfers between devices  52.1 us (8%)
  matrix products  48.7 us (7%)
  other arithmetic  15.1 us (2%)
  local copies, waits for them, and re-layouts  11.5 us (2%)
    all_to_all x4, waiting for transfers between devices, section_layer(): lax.all_to_all(copies, 'expert', split_axis=0, concat_axis=0, tiled=True)  266 us
    all_to_all x4, waiting for transfers between devices, send_back(): lax.all_to_all(partial_value, 'expert', split_axis=0, concat_axis=0, tile...  262 us
    all_to_all x4, starting transfers between devices, section_layer(): lax.all_to_all(copies, 'expert', split_axis=0, concat_axis=0, tiled=True)  30.2 us
    dot_general x4, matrix products, expert_rows(): jnp.dot(activated, down_local, preferred_element_type=jnp.float32)  24.5 us
    all_to_all x4, starting transfers between devices, send_back(): lax.all_to_all(partial_value, 'expert', split_axis=0, concat_axis=0, tile...  21.8 us
    dot_general x4, matrix products, expert_rows(): jnp.dot(token_rows, gate_local, preferred_element_type=jnp.float32)  15.8 us
  transfers between devices with their start and end apart: 10, of which 10 were waited for; matrix products, arithmetic and copies ran while one was open for 8% of the time, Pallas kernels for 0%

commit v1 on v0

v1 whole, which is shorter than its diff:
```python
import jax
import jax.numpy as jnp
from jax import lax
from jax.sharding import PartitionSpec as P

EXPERTS = 8
TICKS = 2
CAP = 24
NX = 4
NZ = 8


def from_behind(block, axis, distance):
    devices = range(lax.axis_size(axis))
    route = [((i - distance) % len(devices), i) for i in devices]
    return lax.ppermute(block, axis, route)


def along_x(block, distance):
    route = [
        (x * NZ + z, ((x + distance) % NX) * NZ + z) for x in range(NX) for z in range(NZ)
    ]
    return lax.ppermute(block, "expert", route)


Z_GROUPS = [[x * NZ + z for z in range(NZ)] for x in range(NX)]


def normed_rows(hidden, gain_row):
    widened = hidden.astype(jnp.float32)
    scale_inv = lax.rsqrt(jnp.mean(widened * widened, axis=-1, keepdims=True) + 1e-06)
    return (widened * scale_inv * gain_row).astype(jnp.bfloat16)


def routing(ids, weights, x_index, half):
    tok = ids.shape[-1]
    wanted = 2 * ((x_index + jnp.arange(NX, dtype=jnp.int32)) % NX) + half
    match = ids[None] == wanted[:, None, None, None]
    weight = jnp.sum(jnp.where(match, weights[None], 0.0), axis=2)
    chosen = jnp.any(match, axis=2)
    count = chosen.astype(jnp.int32)
    rank = jnp.cumsum(count, axis=-1) - count
    slot = jnp.arange(CAP, dtype=jnp.int32)
    hot = chosen[:, :, None, :] & (rank[:, :, None, :] == slot[None, None, :, None])
    same = jnp.eye(NZ, dtype=jnp.bool_)
    block = hot[:, :, :, None, :] & same[None, :, None, :, None]
    pick = block.astype(jnp.bfloat16).reshape(NX * NZ * CAP, NZ * tok)
    high = lax.reduce_precision(weight, 8, 7)
    low = weight - high
    parts = []
    for part in (high, low):
        spread = jnp.where(block, part[:, :, None, None, :], 0.0).astype(jnp.bfloat16)
        parts.append(spread.reshape(NX * NZ * CAP, NZ * tok))
    return pick, parts


def exchange(blocks):
    middle = blocks[2].shape[0] // 2
    one = along_x(blocks[1], 1)
    three = along_x(blocks[3], -1)
    first = along_x(blocks[2][:middle], 1)
    second = along_x(blocks[2][middle:], -1)
    first = along_x(first, 1)
    second = along_x(second, -1)
    return [blocks[0], one, jnp.concatenate([first, second]), three]


def expert_rows(rows, gate_local, up_local, down_local):
    gate_act = jnp.dot(rows, gate_local, preferred_element_type=jnp.float32)
    up_act = jnp.dot(rows, up_local, preferred_element_type=jnp.float32)
    activated = (jax.nn.silu(gate_act) * up_act).astype(jnp.bfloat16)
    return jnp.dot(activated, down_local, preferred_element_type=jnp.float32).astype(jnp.bfloat16)


def gather_z(rows):
    return lax.all_gather(rows, "expert", axis_index_groups=Z_GROUPS, axis=0, tiled=True)


def scatter_z(rows):
    return lax.psum_scatter(
        rows, "expert", scatter_dimension=0, axis_index_groups=Z_GROUPS, tiled=True
    )


def section_layer(hidden, plan, gain_row, gate_local, up_local, down_local):
    pick, parts = plan
    normed = gather_z(normed_rows(hidden, gain_row))
    width = normed.shape[1]
    picked = jnp.dot(pick, normed, preferred_element_type=jnp.float32).astype(jnp.bfloat16)
    rows = jnp.concatenate(exchange(list(picked.reshape(NX, -1, width))))
    out = expert_rows(rows, gate_local, up_local, down_local).reshape(NX, -1, width)
    back = exchange([out[0], out[3], out[2], out[1]])
    back = jnp.concatenate([back[0], back[3], back[2], back[1]])
    dims = (((0,), (0,)), ((), ()))
    moe = sum(
        lax.dot_general(part, back, dims, preferred_element_type=jnp.float32) for part in parts
    )
    moe = scatter_z(moe.astype(jnp.bfloat16))
    return (hidden.astype(jnp.float32) + moe.astype(jnp.float32)).astype(jnp.bfloat16)


def body(
    fwd_state,
    rev_state,
    norm_gain,
    gate_weight,
    up_weight,
    down_weight,
    fwd_routes,
    rev_routes,
    fwd_combine,
    rev_combine,
):
    index = lax.axis_index("expert")
    x_index = index // NZ
    half = (index % NZ) // (NZ // 2)
    gain_row = norm_gain[0]
    weights = (gate_weight[0], up_weight[0], down_weight[0])
    tok = fwd_state.shape[1]
    tables = [a[:, 0].astype(jnp.float32) for a in (fwd_routes, rev_routes, fwd_combine, rev_combine)]
    table = jnp.stack(tables).transpose(0, 1, 3, 2).reshape(-1, tok)
    table = gather_z(table).reshape(NZ, 4, TICKS, 2, tok)
    now = [fwd_state[0], rev_state[0]]
    for tick in range(TICKS):
        nxt = []
        for stream in range(2):
            plan = routing(
                table[:, stream, tick].astype(jnp.int32),
                table[:, 2 + stream, tick],
                x_index,
                half,
            )
            nxt.append(section_layer(now[stream], plan, gain_row, *weights))
        if tick + 1 < TICKS:
            now = [from_behind(nxt[0], "pipe", 1), from_behind(nxt[1], "pipe", -1)]
    return (nxt[0][None], nxt[1][None])


def solution(mesh):
    placed = (
        P("pipe", "expert", None),
        P("pipe", "expert", None),
        P("pipe", None),
        P("pipe", None, "expert"),
        P("pipe", None, "expert"),
        P("pipe", "expert", None),
        P(None, "pipe", "expert", None),
        P(None, "pipe", "expert", None),
        P(None, "pipe", "expert", None),
        P(None, "pipe", "expert", None),
    )
    return jax.shard_map(
        body,
        mesh=mesh,
        in_specs=placed,
        out_specs=(P("pipe", "expert", None), P("pipe", "expert", None)),
        check_vma=False,
    )
```

time: 668 us -> 656 us (0.982)
  the two profiles are of different devices: /device:TPU:32 before, /device:TPU:2 now
where the time goes in v1:
time: 656 us; the launch traced here: 645 us
  waiting for transfers between devices  273 us (42%)
  starting transfers between devices  152 us (23%)
  local copies, waits for them, and re-layouts  78.6 us (12%)
  matrix products  72.9 us (11%)
  blocking collectives  30.9 us (5%)
  other arithmetic  21.3 us (3%)
  between operations  15.8 us (2%)
    ppermute x48, starting transfers between devices, along_x(): return lax.ppermute(block, 'expert', route)  152 us
    all_gather x4, waiting for transfers between devices, gather_z(): lax.all_gather(rows, 'expert', axis_index_groups=Z_GROUPS, axis=0, tiled=...  94.7 us
    reduce_scatter x4, waiting for transfers between devices, scatter_z(): lax.psum_scatter(rows, 'expert', scatter_dimension=0, axis_index_groups=Z...  85.2 us
    ppermute x48, waiting for transfers between devices, along_x(): return lax.ppermute(block, 'expert', route)  85.1 us
    all_gather x1, blocking collectives, gather_z(): lax.all_gather(rows, 'expert', axis_index_groups=Z_GROUPS, axis=0, tiled=...  30.9 us
    dot_general x4, matrix products, expert_rows(): jnp.dot(activated, down_local, preferred_element_type=jnp.float32)  24.4 us
    dot_general x8, matrix products, section_layer(): lax.dot_general(part, back, dims, preferred_element_type=jnp.float32)  24.4 us
    unnamed x98, local copies, waits for them, and re-layouts  24.2 us
  transfers between devices with their start and end apart: 58, of which 25 were waited for; matrix products, arithmetic and copies ran while one was open for 23% of the time, Pallas kernels for 0%

profile of v1, /device:TPU:2, one launch (start us, length us, event | category | flops | bytes accessed | tf_op | source)
XLA Modules:
  0.0 644.8 jit_solution(5164950612043724849)
XLA Ops:
  13.8 30.9 %all_gather.15 = f32[128,64]{1,0:T(8,128)S(1)} all-gather(f32[16,64]{1,0:T(8,128)S(1)} %bitcast.151), channel_id=1, replica_groups={{0,1,2,3,4,5,6,7},{8,9,10,11,12,13,14,15},{16,17,18,19,20,21,22,23},{24..., dimensions={0}, use_global_device_ids=true | all-gather | bytes 36864 | tf_op jit(solution)/shard_map/all_gather | solution.py:76
  48.9 3.4 broadcast_and_fusion.1
  61.0 3.5 convolution_convert_fusion.1
  67.5 3.4 collective-permute-start.25
  70.9 35.2 %all-gather.5.cloned.1.call-done = bf16[512,2048]{1,0:T(8,128)(2,1)} async-done(((bf16[64,2048]{1,0:T(8,128)(2,1)}), bf16[512,2048]{1,0:T(8,128)(2,1)}) %all-gather.5.cloned.1.call-update) | async-done | bytes 2097168 | tf_op jit(solution)/shard_map/all_gather | solution.py:76
  106.1 3.4 convolution_convert_fusion.3
  109.7 3.5 collective-permute-start
  114.4 3.1 collective-permute-start.26
  120.3 3.7 collective-permute-start.30
  124.1 11.9 %collective-permute-done.26 = bf16[96,2048]{1,0:T(8,128)(2,1)S(1)} collective-permute-done((bf16[96,2048]{1,0:T(8,128)(2,1)S(1)}, bf16[96,2048]{1,0:T(8,128)(2,1)S(1)}, u32[]{:S(2)}, u32[]{:S(2)}) %collective-permute-start.26) | collective-permute-done | bytes 393248 | tf_op jit(solution)/shard_map/ppermute | solution.py:23
  136.0 3.4 collective-permute-start.1
  141.8 3.4 collective-permute-start.27
  146.5 3.3 collective-permute-start.29
  150.0 5.1 collective-permute-start.5
  157.6 4.1 collective-permute-start.4
  167.8 6.2 convolution_convert_fusion.5
  175.8 3.0 collective-permute-start.31
  182.8 3.0 collective-permute-start.34
  193.1 4.3 collective-permute-start.33
  199.5 11.0 %collective-permute-done.34 = bf16[96,2048]{1,0:T(8,128)(2,1)S(1)} collective-permute-done((bf16[96,2048]{1,0:T(8,128)(2,1)S(1)}, bf16[96,2048]{1,0:T(8,128)(2,1)S(1)}, u32[]{:S(2)}, u32[]{:S(2)}) %collective-permute-start.34) | collective-permute-done | bytes 393248 | tf_op jit(solution)/shard_map/ppermute | solution.py:23
  215.0 5.1 collective-permute-done.35
  222.1 3.3 add_convert_fusion.1
  225.4 3.1 fusion.14
  228.6 6.0 convolution_convert_fusion.7
  234.6 3.1 fusion.111
  237.7 3.4 collective-permute-start.6
  245.5 5.2 collective-permute-start.9
  252.6 4.4 collective-permute-done.7
  264.0 4.9 collective-permute-start.10
  271.1 8.8 %collective-permute-done.8 = bf16[96,2048]{1,0:T(8,128)(2,1)} collective-permute-done((bf16[96,2048]{1,0:T(8,128)(2,1)}, bf16[96,2048]{1,0:T(8,128)(2,1)}, u32[]{:S(2)}, u32[]{:S(2)}) %collective-permute-start.8) | collective-permute-done | bytes 393248 | tf_op jit(solution)/shard_map/ppermute | solution.py:23
  284.5 3.9 fusion
  288.5 3.2 add_convert_fusion.3
  292.9 43.0 %reduce-scatter.5.cloned.1.call-done = bf16[64,2048]{1,0:T(8,128)(2,1)} async-done(((bf16[512,2048]{1,0:T(8,128)(2,1)}), bf16[64,2048]{1,0:T(8,128)(2,1)}) %reduce-scatter.5.cloned.1.call-update) | async-done | bytes 262160 | tf_op jit(solution)/shard_map/reduce_scatter | solution.py:80
  337.1 6.8 %collective-permute-done.12 = bf16[64,2048]{1,0:T(8,128)(2,1)S(1)} collective-permute-done((bf16[64,2048]{1,0:T(8,128)(2,1)S(1)}, bf16[64,2048]{1,0:T(8,128)(2,1)S(1)}, u32[]{:S(2)}, u32[]{:S(2)}) %collective-permute-start.12) | collective-permute-done | bytes 262176 | tf_op jit(solution)/shard_map/ppermute | solution.py:16
  353.7 34.0 %all-gather.7.cloned.1.call-done = bf16[512,2048]{1,0:T(8,128)(2,1)} async-done(((bf16[64,2048]{1,0:T(8,128)(2,1)}), bf16[512,2048]{1,0:T(8,128)(2,1)}) %all-gather.7.cloned.1.call-update) | async-done | bytes 2097168 | tf_op jit(solution)/shard_map/all_gather | solution.py:76
  387.8 3.5 convolution_convert_fusion.2
  392.7 3.4 collective-permute-start.13
  397.1 3.1 collective-permute-start.14
  402.9 4.1 collective-permute-start.18
  407.0 25.5 %all-gather.11.cloned.1.call-done = bf16[512,2048]{1,0:T(8,128)(2,1)} async-done(((bf16[64,2048]{1,0:T(8,128)(2,1)}), bf16[512,2048]{1,0:T(8,128)(2,1)}) %all-gather.11.cloned.1.call-update) | async-done | bytes 2097168 | tf_op jit(solution)/shard_map/all_gather | solution.py:76
  432.5 3.4 convolution_convert_fusion
  437.3 3.5 collective-permute-start.15
  440.9 3.4 collective-permute-start.39
  446.8 3.7 collective-permute-start.17
  451.7 3.3 collective-permute-start.38
  455.1 4.0 collective-permute-done.39
  459.1 3.7 collective-permute-start.43
  474.4 6.2 convolution_convert_fusion.6
  483.6 5.1 collective-permute-start.19
  491.9 3.9 collective-permute-start.22
  505.9 6.8 %collective-permute-done.22 = bf16[96,2048]{1,0:T(8,128)(2,1)S(1)} collective-permute-done((bf16[96,2048]{1,0:T(8,128)(2,1)S(1)}, bf16[96,2048]{1,0:T(8,128)(2,1)S(1)}, u32[]{:S(2)}, u32[]{:S(2)}) %collective-permute-start.22) | collective-permute-done | bytes 393248 | tf_op jit(solution)/shard_map/ppermute | solution.py:23
  515.2 4.2 collective-permute-done.21
  524.3 3.3 add_convert_fusion.2
  527.8 3.1 fusion.8
  530.9 6.0 convolution_convert_fusion.4
  537.0 3.1 fusion.99
  544.4 3.4 collective-permute-start.45
  547.8 4.0 collective-permute-start.47
  553.8 6.1 collective-permute-done.45
  566.0 4.2 collective-permute-start.48
  572.4 8.0 %collective-permute-done.46 = bf16[96,2048]{1,0:T(8,128)(2,1)} collective-permute-done((bf16[96,2048]{1,0:T(8,128)(2,1)}, bf16[96,2048]{1,0:T(8,128)(2,1)}, u32[]{:S(2)}, u32[]{:S(2)}) %collective-permute-start.46) | collective-permute-done | bytes 393248 | tf_op jit(solution)/shard_map/ppermute | solution.py:23
  585.1 3.9 fusion.3
  589.0 3.2 add_convert_fusion
  593.9 42.1 %reduce-scatter.11.cloned.1.call-done = bf16[64,2048]{1,0:T(8,128)(2,1)} async-done(((bf16[512,2048]{1,0:T(8,128)(2,1)}), bf16[64,2048]{1,0:T(8,128)(2,1)}) %reduce-scatter.11.cloned.1.call-update) | async-done | bytes 262160 | tf_op jit(solution)/shard_map/reduce_scatter | solution.py:80
  (268 shorter events, 160.8 us)
Async XLA Ops:
  7.2 160.7 %copy-start = (bf16[1,192,2048]{2,1,0:T(8,128)(2,1)S(1)}, bf16[1,192,2048]{2,1,0:T(8,128)(2,1)}, u32[]{:S(2)}) copy-start(bf16[1,192,2048]{2,1,0:T(8,128)(2,1)} %param.15) | copy-start | bytes 2359300
  7.2 53.8 %all-gather.9.cloned.1.call-start = ((), (), s32[]{:S(2)}) async-start(), calls=%async_computation.8 | async-start | bytes 2359296 | tf_op jit(solution)/shard_map/all_gather | solution.py:76
  11.6 94.5 %all-gather.5.cloned.1.call-start = ((), (), s32[]{:S(2)}) async-start(), calls=%async_computation.4 | async-start | bytes 2359296 | tf_op jit(solution)/shard_map/all_gather | solution.py:76
  12.3 279.4 %reduce-scatter.9.cloned.1.call-start = ((), (), s32[]{:S(2)}) async-start(), calls=%async_computation.9 | async-start | bytes 2359296 | tf_op jit(solution)/shard_map/reduce_scatter | solution.py:80
  67.5 74.3 %collective-permute-start.25 = (bf16[192,2048]{1,0:T(8,128)(2,1)}, bf16[192,2048]{1,0:T(8,128)(2,1)}, u32[]{:S(2)}, u32[]{:S(2)}) collective-permute-start(bf16[192,2048]{1,0:T(8,128)(2,1)} %get-tuple-element.26), channel_id=1, source_target_pairs={{0,8},{1,9},{2,10},{3,11},{4,12},{5,13},{6,14},{7,15},{8,16},{9,17... | collective-permute-start | bytes 2359304 | tf_op jit(solution)/shard_map/ppermute | solution.py:23
  109.7 36.8 %collective-permute-start = (bf16[192,2048]{1,0:T(8,128)(2,1)S(1)}, bf16[192,2048]{1,0:T(8,128)(2,1)S(1)}, u32[]{:S(2)}, u32[]{:S(2)}) collective-permute-start(bf16[192,2048]{1,0:T(8,128)(2,1)S(1)} %get-tuple-element.46), channel_id=1, source_target_pairs={{0,8},{1,9},{2,10},{3,11},{4,12},{5,13},{6,14},{7,15},{8,16},{9,17... | collective-permute-start | bytes 2359304 | tf_op jit(solution)/shard_map/ppermute | solution.py:23
  114.4 21.5 %collective-permute-start.26 = (bf16[96,2048]{1,0:T(8,128)(2,1)S(1)}, bf16[96,2048]{1,0:T(8,128)(2,1)S(1)}, u32[]{:S(2)}, u32[]{:S(2)}) collective-permute-start(bf16[96,2048]{1,0:T(8,128)(2,1)S(1)} %get-tuple-element.29), channel_id=1, source_target_pairs={{0,8},{1,9},{2,10},{3,11},{4,12},{5,13},{6,14},{7,15},{8,16},{9,17... | collective-permute-start | bytes 1179656 | tf_op jit(solution)/shard_map/ppermute | solution.py:23
  117.5 21.9 %collective-permute-start.28 = (bf16[96,2048]{1,0:T(8,128)(2,1)S(1)}, bf16[96,2048]{1,0:T(8,128)(2,1)S(1)}, u32[]{:S(2)}, u32[]{:S(2)}) collective-permute-start(bf16[96,2048]{1,0:T(8,128)(2,1)S(1)} %get-tuple-element.28), channel_id=1, source_target_pairs={{0,24},{1,25},{2,26},{3,27},{4,28},{5,29},{6,30},{7,31},{8,0},{9,1... | collective-permute-start | bytes 1179656 | tf_op jit(solution)/shard_map/ppermute | solution.py:23
  120.3 43.7 %collective-permute-start.30 = (bf16[192,2048]{1,0:T(8,128)(2,1)S(1)}, bf16[192,2048]{1,0:T(8,128)(2,1)S(1)}, u32[]{:S(2)}, u32[]{:S(2)}) collective-permute-start(bf16[192,2048]{1,0:T(8,128)(2,1)S(1)} %get-tuple-element.25), channel_id=1, source_target_pairs={{0,24},{1,25},{2,26},{3,27},{4,28},{5,29},{6,30},{7,31},{8,0},{9,1... | collective-permute-start | bytes 2359304 | tf_op jit(solution)/shard_map/ppermute | solution.py:23
  136.0 14.0 %collective-permute-start.1 = (bf16[96,2048]{1,0:T(8,128)(2,1)S(1)}, bf16[96,2048]{1,0:T(8,128)(2,1)}, u32[]{:S(2)}, u32[]{:S(2)}) collective-permute-start(bf16[96,2048]{1,0:T(8,128)(2,1)S(1)} %get-tuple-element.49), channel_id=1, source_target_pairs={{0,8},{1,9},{2,10},{3,11},{4,12},{5,13},{6,14},{7,15},{8,16},{9,17... | collective-permute-start | bytes 1179656 | tf_op jit(solution)/shard_map/ppermute | solution.py:23
  139.4 16.2 %collective-permute-start.3 = (bf16[96,2048]{1,0:T(8,128)(2,1)S(1)}, bf16[96,2048]{1,0:T(8,128)(2,1)}, u32[]{:S(2)}, u32[]{:S(2)}) collective-permute-start(bf16[96,2048]{1,0:T(8,128)(2,1)S(1)} %get-tuple-element.48), channel_id=1, source_target_pairs={{0,24},{1,25},{2,26},{3,27},{4,28},{5,29},{6,30},{7,31},{8,0},{9,1... | collective-permute-start | bytes 1179656 | tf_op jit(solution)/shard_map/ppermute | solution.py:23
  141.8 15.7 %collective-permute-start.27 = (bf16[96,2048]{1,0:T(8,128)(2,1)S(1)}, bf16[96,2048]{1,0:T(8,128)(2,1)S(1)}, u32[]{:S(2)}, u32[]{:S(2)}) collective-permute-start(bf16[96,2048]{1,0:T(8,128)(2,1)S(1)} %collective-permute-done.26), channel_id=1, source_target_pairs={{0,8},{1,9},{2,10},{3,11},{4,12},{5,13},{6,14},{7,15},{8,16},{9,17... | collective-permute-start | bytes 1179656 | tf_op jit(solution)/shard_map/ppermute | solution.py:23
  146.5 17.4 %collective-permute-start.29 = (bf16[96,2048]{1,0:T(8,128)(2,1)S(1)}, bf16[96,2048]{1,0:T(8,128)(2,1)S(1)}, u32[]{:S(2)}, u32[]{:S(2)}) collective-permute-start(bf16[96,2048]{1,0:T(8,128)(2,1)S(1)} %collective-permute-done.28), channel_id=1, source_target_pairs={{0,24},{1,25},{2,26},{3,27},{4,28},{5,29},{6,30},{7,31},{8,0},{9,1... | collective-permute-start | bytes 1179656 | tf_op jit(solution)/shard_map/ppermute | solution.py:23
  150.0 47.4 %collective-permute-start.5 = (bf16[192,2048]{1,0:T(8,128)(2,1)S(1)}, bf16[192,2048]{1,0:T(8,128)(2,1)}, u32[]{:S(2)}, u32[]{:S(2)}) collective-permute-start(bf16[192,2048]{1,0:T(8,128)(2,1)S(1)} %get-tuple-element.45), channel_id=1, source_target_pairs={{0,24},{1,25},{2,26},{3,27},{4,28},{5,29},{6,30},{7,31},{8,0},{9,1... | collective-permute-start | bytes 2359304 | tf_op jit(solution)/shard_map/ppermute | solution.py:23
  155.6 27.2 %collective-permute-start.2 = (bf16[96,2048]{1,0:T(8,128)(2,1)}, bf16[96,2048]{1,0:T(8,128)(2,1)}, u32[]{:S(2)}, u32[]{:S(2)}) collective-permute-start(bf16[96,2048]{1,0:T(8,128)(2,1)} %collective-permute-done.1), channel_id=1, source_target_pairs={{0,8},{1,9},{2,10},{3,11},{4,12},{5,13},{6,14},{7,15},{8,16},{9,17... | collective-permute-start | bytes 1179656 | tf_op jit(solution)/shard_map/ppermute | solution.py:23
  157.6 31.8 %collective-permute-start.4 = (bf16[96,2048]{1,0:T(8,128)(2,1)}, bf16[96,2048]{1,0:T(8,128)(2,1)}, u32[]{:S(2)}, u32[]{:S(2)}) collective-permute-start(bf16[96,2048]{1,0:T(8,128)(2,1)} %collective-permute-done.3), channel_id=1, source_target_pairs={{0,24},{1,25},{2,26},{3,27},{4,28},{5,29},{6,30},{7,31},{8,0},{9,1... | collective-permute-start | bytes 1179656 | tf_op jit(solution)/shard_map/ppermute | solution.py:23
  175.8 37.4 %collective-permute-start.31 = (bf16[192,2048]{1,0:T(8,128)(2,1)S(1)}, bf16[192,2048]{1,0:T(8,128)(2,1)S(1)}, u32[]{:S(2)}, u32[]{:S(2)}) collective-permute-start(bf16[192,2048]{1,0:T(8,128)(2,1)S(1)} %get-tuple-element.21), channel_id=1, source_target_pairs={{0,24},{1,25},{2,26},{3,27},{4,28},{5,29},{6,30},{7,31},{8,0},{9,1... | collective-permute-start | bytes 2359304 | tf_op jit(solution)/shard_map/ppermute | solution.py:23
  180.0 13.1 %collective-permute-start.32 = (bf16[96,2048]{1,0:T(8,128)(2,1)S(1)}, bf16[96,2048]{1,0:T(8,128)(2,1)S(1)}, u32[]{:S(2)}, u32[]{:S(2)}) collective-permute-start(bf16[96,2048]{1,0:T(8,128)(2,1)S(1)} %get-tuple-element.24), channel_id=1, source_target_pairs={{0,8},{1,9},{2,10},{3,11},{4,12},{5,13},{6,14},{7,15},{8,16},{9,17... | collective-permute-start | bytes 1179656 | tf_op jit(solution)/shard_map/ppermute | solution.py:23
  182.8 27.6 %collective-permute-start.34 = (bf16[96,2048]{1,0:T(8,128)(2,1)S(1)}, bf16[96,2048]{1,0:T(8,128)(2,1)S(1)}, u32[]{:S(2)}, u32[]{:S(2)}) collective-permute-start(bf16[96,2048]{1,0:T(8,128)(2,1)S(1)} %get-tuple-element.23), channel_id=1, source_target_pairs={{0,24},{1,25},{2,26},{3,27},{4,28},{5,29},{6,30},{7,31},{8,0},{9,1... | collective-permute-start | bytes 1179656 | tf_op jit(solution)/shard_map/ppermute | solution.py:23
  189.3 30.8 %collective-permute-start.36 = (bf16[192,2048]{1,0:T(8,128)(2,1)S(1)}, bf16[192,2048]{1,0:T(8,128)(2,1)S(1)}, u32[]{:S(2)}, u32[]{:S(2)}) collective-permute-start(bf16[192,2048]{1,0:T(8,128)(2,1)S(1)} %get-tuple-element.20), channel_id=1, source_target_pairs={{0,8},{1,9},{2,10},{3,11},{4,12},{5,13},{6,14},{7,15},{8,16},{9,17... | collective-permute-start | bytes 2359304 | tf_op jit(solution)/shard_map/ppermute | solution.py:23
  193.1 21.9 %collective-permute-start.33 = (bf16[96,2048]{1,0:T(8,128)(2,1)S(1)}, bf16[96,2048]{1,0:T(8,128)(2,1)S(1)}, u32[]{:S(2)}, u32[]{:S(2)}) collective-permute-start(bf16[96,2048]{1,0:T(8,128)(2,1)S(1)} %collective-permute-done.32), channel_id=1, source_target_pairs={{0,8},{1,9},{2,10},{3,11},{4,12},{5,13},{6,14},{7,15},{8,16},{9,17... | collective-permute-start | bytes 1179656 | tf_op jit(solution)/shard_map/ppermute | solution.py:23
  210.4 9.7 %collective-permute-start.35 = (bf16[96,2048]{1,0:T(8,128)(2,1)S(1)}, bf16[96,2048]{1,0:T(8,128)(2,1)S(1)}, u32[]{:S(2)}, u32[]{:S(2)}) collective-permute-start(bf16[96,2048]{1,0:T(8,128)(2,1)S(1)} %collective-permute-done.34), channel_id=1, source_target_pairs={{0,24},{1,25},{2,26},{3,27},{4,28},{5,29},{6,30},{7,31},{8,0},{9,1... | collective-permute-start | bytes 1179656 | tf_op jit(solution)/shard_map/ppermute | solution.py:23
  225.4 110.5 %reduce-scatter.5.cloned.1.call-start = ((), (), s32[]{:S(2)}) async-start(), calls=%async_computation.5 | async-start | bytes 2359296 | tf_op jit(solution)/shard_map/reduce_scatter | solution.py:80
  237.7 31.2 %collective-permute-start.6 = (bf16[192,2048]{1,0:T(8,128)(2,1)}, bf16[192,2048]{1,0:T(8,128)(2,1)}, u32[]{:S(2)}, u32[]{:S(2)}) collective-permute-start(bf16[192,2048]{1,0:T(8,128)(2,1)} %get-tuple-element.41), channel_id=1, source_target_pairs={{0,24},{1,25},{2,26},{3,27},{4,28},{5,29},{6,30},{7,31},{8,0},{9,1... | collective-permute-start | bytes 2359304 | tf_op jit(solution)/shard_map/ppermute | solution.py:23
  243.1 13.9 %collective-permute-start.7 = (bf16[96,2048]{1,0:T(8,128)(2,1)S(1)}, bf16[96,2048]{1,0:T(8,128)(2,1)}, u32[]{:S(2)}, u32[]{:S(2)}) collective-permute-start(bf16[96,2048]{1,0:T(8,128)(2,1)S(1)} %get-tuple-element.44), channel_id=1, source_target_pairs={{0,8},{1,9},{2,10},{3,11},{4,12},{5,13},{6,14},{7,15},{8,16},{9,17... | collective-permute-start | bytes 1179656 | tf_op jit(solution)/shard_map/ppermute | solution.py:23
  245.5 18.5 %collective-permute-start.9 = (bf16[96,2048]{1,0:T(8,128)(2,1)}, bf16[96,2048]{1,0:T(8,128)(2,1)}, u32[]{:S(2)}, u32[]{:S(2)}) collective-permute-start(bf16[96,2048]{1,0:T(8,128)(2,1)} %get-tuple-element.43), channel_id=1, source_target_pairs={{0,24},{1,25},{2,26},{3,27},{4,28},{5,29},{6,30},{7,31},{8,0},{9,1... | collective-permute-start | bytes 1179656 | tf_op jit(solution)/shard_map/ppermute | solution.py:23
  250.7 31.8 %collective-permute-start.11 = (bf16[192,2048]{1,0:T(8,128)(2,1)}, bf16[192,2048]{1,0:T(8,128)(2,1)}, u32[]{:S(2)}, u32[]{:S(2)}) collective-permute-start(bf16[192,2048]{1,0:T(8,128)(2,1)} %get-tuple-element.40), channel_id=1, source_target_pairs={{0,8},{1,9},{2,10},{3,11},{4,12},{5,13},{6,14},{7,15},{8,16},{9,17... | collective-permute-start | bytes 2359304 | tf_op jit(solution)/shard_map/ppermute | solution.py:23
  257.0 22.8 %collective-permute-start.8 = (bf16[96,2048]{1,0:T(8,128)(2,1)}, bf16[96,2048]{1,0:T(8,128)(2,1)}, u32[]{:S(2)}, u32[]{:S(2)}) collective-permute-start(bf16[96,2048]{1,0:T(8,128)(2,1)} %collective-permute-done.7), channel_id=1, source_target_pairs={{0,8},{1,9},{2,10},{3,11},{4,12},{5,13},{6,14},{7,15},{8,16},{9,17... | collective-permute-start | bytes 1179656 | tf_op jit(solution)/shard_map/ppermute | solution.py:23
  264.0 17.6 %collective-permute-start.10 = (bf16[96,2048]{1,0:T(8,128)(2,1)}, bf16[96,2048]{1,0:T(8,128)(2,1)S(1)}, u32[]{:S(2)}, u32[]{:S(2)}) collective-permute-start(bf16[96,2048]{1,0:T(8,128)(2,1)} %collective-permute-done.9), channel_id=1, source_target_pairs={{0,24},{1,25},{2,26},{3,27},{4,28},{5,29},{6,30},{7,31},{8,0},{9,1... | collective-permute-start | bytes 1179656 | tf_op jit(solution)/shard_map/ppermute | solution.py:23
  288.5 47.4 %copy-start.6 = (bf16[1,64,2048]{2,1,0:T(8,128)(2,1)S(1)}, bf16[1,64,2048]{2,1,0:T(8,128)(2,1)}, u32[]{:S(2)}) copy-start(bf16[1,64,2048]{2,1,0:T(8,128)(2,1)} %param.10) | copy-start | bytes 786436
  291.6 52.4 %copy-start.26 = (f32[1,2048]{1,0:T(1,128)S(1)}, f32[1,2048]{1,0:T(1,128)}, u32[]{:S(2)}) copy-start(f32[1,2048]{1,0:T(1,128)} %param.12) | copy-start | bytes 24580
  291.6 54.1 %copy-start.4 = (pred[4,8,24,8,64]{4,3,2,1,0:T(8,128)(4,1)S(1)}, pred[4,8,24,8,64]{4,3,2,1,0:T(8,128)(4,1)}, u32[]{:S(2)}) copy-start(pred[4,8,24,8,64]{4,3,2,1,0:T(8,128)(4,1)} %get-tuple-element.71) | copy-start | bytes 1179652
  291.6 56.3 %copy-start.24 = (f32[4,8,64]{2,1,0:T(8,128)S(1)}, f32[4,8,64]{2,1,0:T(8,128)}, u32[]{:S(2)}) copy-start(f32[4,8,64]{2,1,0:T(8,128)} %get-tuple-element.4) | copy-start | bytes 24580
  291.7 96.1 %all-gather.7.cloned.1.call-start = ((), (), s32[]{:S(2)}) async-start(), calls=%async_computation.6 | async-start | bytes 2359296 | tf_op jit(solution)/shard_map/all_gather | solution.py:76
  292.8 44.1 %collective-permute-start.37 = (bf16[64,2048]{1,0:T(8,128)(2,1)S(1)}, bf16[64,2048]{1,0:T(8,128)(2,1)S(1)}, u32[]{:S(2)}, u32[]{:S(2)}) collective-permute-start(bf16[64,2048]{1,0:T(8,128)(2,1)S(1)} %fusion.47), channel_id=1, source_target_pairs={{32,0},{64,32},{96,64},{128,96},{160,128},{192,160},{224,192},{256... | collective-permute-start | bytes 786440 | tf_op jit(solution)/shard_map/ppermute | solution.py:16
  336.9 7.0 %collective-permute-start.12 = (bf16[64,2048]{1,0:T(8,128)(2,1)S(1)}, bf16[64,2048]{1,0:T(8,128)(2,1)S(1)}, u32[]{:S(2)}, u32[]{:S(2)}) collective-permute-start(bf16[64,2048]{1,0:T(8,128)(2,1)S(1)} %fusion.43), channel_id=1, source_target_pairs={{480,0},{0,32},{32,64},{64,96},{96,128},{128,160},{160,192},{192,2... | collective-permute-start | bytes 786440 | tf_op jit(solution)/shard_map/ppermute | solution.py:16
  345.1 87.4 %all-gather.11.cloned.1.call-start = ((), (), s32[]{:S(2)}) async-start(), calls=%async_computation.10 | async-start | bytes 2359296 | tf_op jit(solution)/shard_map/all_gather | solution.py:76
  345.7 246.5 %reduce-scatter.7.cloned.1.call-start = ((), (), s32[]{:S(2)}) async-start(), calls=%async_computation.7 | async-start | bytes 2359296 | tf_op jit(solution)/shard_map/reduce_scatter | solution.py:80
  353.7 78.8 %copy-start.9 = (pred[768,512]{1,0:T(32,128)(4,1)}, pred[768,512]{1,0:T(32,128)(4,1)S(1)}, u32[]{:S(2)}) copy-start(pred[768,512]{1,0:T(32,128)(4,1)S(1)} %and.178) | copy-start | bytes 1179652
  392.7 54.1 %collective-permute-start.13 = (bf16[192,2048]{1,0:T(8,128)(2,1)}, bf16[192,2048]{1,0:T(8,128)(2,1)}, u32[]{:S(2)}, u32[]{:S(2)}) collective-permute-start(bf16[192,2048]{1,0:T(8,128)(2,1)} %get-tuple-element.36), channel_id=1, source_target_pairs={{0,8},{1,9},{2,10},{3,11},{4,12},{5,13},{6,14},{7,15},{8,16},{9,17... | collective-permute-start | bytes 2359304 | tf_op jit(solution)/shard_map/ppermute | solution.py:23
  397.1 40.3 %collective-permute-start.14 = (bf16[96,2048]{1,0:T(8,128)(2,1)}, bf16[96,2048]{1,0:T(8,128)(2,1)}, u32[]{:S(2)}, u32[]{:S(2)}) collective-permute-start(bf16[96,2048]{1,0:T(8,128)(2,1)} %get-tuple-element.39), channel_id=1, source_target_pairs={{0,8},{1,9},{2,10},{3,11},{4,12},{5,13},{6,14},{7,15},{8,16},{9,17... | collective-permute-start | bytes 1179656 | tf_op jit(solution)/shard_map/ppermute | solution.py:23
  400.2 44.2 %collective-permute-start.16 = (bf16[96,2048]{1,0:T(8,128)(2,1)}, bf16[96,2048]{1,0:T(8,128)(2,1)}, u32[]{:S(2)}, u32[]{:S(2)}) collective-permute-start(bf16[96,2048]{1,0:T(8,128)(2,1)} %get-tuple-element.38), channel_id=1, source_target_pairs={{0,24},{1,25},{2,26},{3,27},{4,28},{5,29},{6,30},{7,31},{8,0},{9,1... | collective-permute-start | bytes 1179656 | tf_op jit(solution)/shard_map/ppermute | solution.py:23
  402.9 66.4 %collective-permute-start.18 = (bf16[192,2048]{1,0:T(8,128)(2,1)S(1)}, bf16[192,2048]{1,0:T(8,128)(2,1)}, u32[]{:S(2)}, u32[]{:S(2)}) collective-permute-start(bf16[192,2048]{1,0:T(8,128)(2,1)S(1)} %get-tuple-element.35), channel_id=1, source_target_pairs={{0,24},{1,25},{2,26},{3,27},{4,28},{5,29},{6,30},{7,31},{8,0},{9,1... | collective-permute-start | bytes 2359304 | tf_op jit(solution)/shard_map/ppermute | solution.py:23
  437.3 14.3 %collective-permute-start.15 = (bf16[96,2048]{1,0:T(8,128)(2,1)}, bf16[96,2048]{1,0:T(8,128)(2,1)S(1)}, u32[]{:S(2)}, u32[]{:S(2)}) collective-permute-start(bf16[96,2048]{1,0:T(8,128)(2,1)} %collective-permute-done.14), channel_id=1, source_target_pairs={{0,8},{1,9},{2,10},{3,11},{4,12},{5,13},{6,14},{7,15},{8,16},{9,17... | collective-permute-start | bytes 1179656 | tf_op jit(solution)/shard_map/ppermute | solution.py:23
  440.9 18.2 %collective-permute-start.39 = (bf16[96,2048]{1,0:T(8,128)(2,1)S(1)}, bf16[96,2048]{1,0:T(8,128)(2,1)}, u32[]{:S(2)}, u32[]{:S(2)}) collective-permute-start(bf16[96,2048]{1,0:T(8,128)(2,1)S(1)} %get-tuple-element.19), channel_id=1, source_target_pairs={{0,8},{1,9},{2,10},{3,11},{4,12},{5,13},{6,14},{7,15},{8,16},{9,17... | collective-permute-start | bytes 1179656 | tf_op jit(solution)/shard_map/ppermute | solution.py:23
  444.4 18.4 %collective-permute-start.41 = (bf16[96,2048]{1,0:T(8,128)(2,1)S(1)}, bf16[96,2048]{1,0:T(8,128)(2,1)}, u32[]{:S(2)}, u32[]{:S(2)}) collective-permute-start(bf16[96,2048]{1,0:T(8,128)(2,1)S(1)} %get-tuple-element.18), channel_id=1, source_target_pairs={{0,24},{1,25},{2,26},{3,27},{4,28},{5,29},{6,30},{7,31},{8,0},{9,1... | collective-permute-start | bytes 1179656 | tf_op jit(solution)/shard_map/ppermute | solution.py:23
  446.8 19.9 %collective-permute-start.17 = (bf16[96,2048]{1,0:T(8,128)(2,1)}, bf16[96,2048]{1,0:T(8,128)(2,1)S(1)}, u32[]{:S(2)}, u32[]{:S(2)}) collective-permute-start(bf16[96,2048]{1,0:T(8,128)(2,1)} %collective-permute-done.16), channel_id=1, source_target_pairs={{0,24},{1,25},{2,26},{3,27},{4,28},{5,29},{6,30},{7,31},{8,0},{9,1... | collective-permute-start | bytes 1179656 | tf_op jit(solution)/shard_map/ppermute | solution.py:23
  451.7 37.1 %collective-permute-start.38 = (bf16[192,2048]{1,0:T(8,128)(2,1)}, bf16[192,2048]{1,0:T(8,128)(2,1)}, u32[]{:S(2)}, u32[]{:S(2)}) collective-permute-start(bf16[192,2048]{1,0:T(8,128)(2,1)} %get-tuple-element.16), channel_id=1, source_target_pairs={{0,8},{1,9},{2,10},{3,11},{4,12},{5,13},{6,14},{7,15},{8,16},{9,17... | collective-permute-start | bytes 2359304 | tf_op jit(solution)/shard_map/ppermute | solution.py:23
  459.1 45.6 %collective-permute-start.43 = (bf16[192,2048]{1,0:T(8,128)(2,1)S(1)}, bf16[192,2048]{1,0:T(8,128)(2,1)}, u32[]{:S(2)}, u32[]{:S(2)}) collective-permute-start(bf16[192,2048]{1,0:T(8,128)(2,1)S(1)} %get-tuple-element.15), channel_id=1, source_target_pairs={{0,24},{1,25},{2,26},{3,27},{4,28},{5,29},{6,30},{7,31},{8,0},{9,1... | collective-permute-start | bytes 2359304 | tf_op jit(solution)/shard_map/ppermute | solution.py:23
  462.8 29.2 %collective-permute-start.40 = (bf16[96,2048]{1,0:T(8,128)(2,1)}, bf16[96,2048]{1,0:T(8,128)(2,1)}, u32[]{:S(2)}, u32[]{:S(2)}) collective-permute-start(bf16[96,2048]{1,0:T(8,128)(2,1)} %collective-permute-done.39), channel_id=1, source_target_pairs={{0,8},{1,9},{2,10},{3,11},{4,12},{5,13},{6,14},{7,15},{8,16},{9,17... | collective-permute-start | bytes 1179656 | tf_op jit(solution)/shard_map/ppermute | solution.py:23
  466.7 30.2 %collective-permute-start.42 = (bf16[96,2048]{1,0:T(8,128)(2,1)}, bf16[96,2048]{1,0:T(8,128)(2,1)}, u32[]{:S(2)}, u32[]{:S(2)}) collective-permute-start(bf16[96,2048]{1,0:T(8,128)(2,1)} %collective-permute-done.41), channel_id=1, source_target_pairs={{0,24},{1,25},{2,26},{3,27},{4,28},{5,29},{6,30},{7,31},{8,0},{9,1... | collective-permute-start | bytes 1179656 | tf_op jit(solution)/shard_map/ppermute | solution.py:23
  483.6 31.4 %collective-permute-start.19 = (bf16[192,2048]{1,0:T(8,128)(2,1)S(1)}, bf16[192,2048]{1,0:T(8,128)(2,1)S(1)}, u32[]{:S(2)}, u32[]{:S(2)}) collective-permute-start(bf16[192,2048]{1,0:T(8,128)(2,1)S(1)} %get-tuple-element.31), channel_id=1, source_target_pairs={{0,24},{1,25},{2,26},{3,27},{4,28},{5,29},{6,30},{7,31},{8,0},{9,1... | collective-permute-start | bytes 2359304 | tf_op jit(solution)/shard_map/ppermute | solution.py:23
  488.8 13.9 %collective-permute-start.20 = (bf16[96,2048]{1,0:T(8,128)(2,1)S(1)}, bf16[96,2048]{1,0:T(8,128)(2,1)S(1)}, u32[]{:S(2)}, u32[]{:S(2)}) collective-permute-start(bf16[96,2048]{1,0:T(8,128)(2,1)S(1)} %get-tuple-element.34), channel_id=1, source_target_pairs={{0,8},{1,9},{2,10},{3,11},{4,12},{5,13},{6,14},{7,15},{8,16},{9,17... | collective-permute-start | bytes 1179656 | tf_op jit(solution)/shard_map/ppermute | solution.py:23
  491.9 20.7 %collective-permute-start.22 = (bf16[96,2048]{1,0:T(8,128)(2,1)S(1)}, bf16[96,2048]{1,0:T(8,128)(2,1)S(1)}, u32[]{:S(2)}, u32[]{:S(2)}) collective-permute-start(bf16[96,2048]{1,0:T(8,128)(2,1)S(1)} %get-tuple-element.33), channel_id=1, source_target_pairs={{0,24},{1,25},{2,26},{3,27},{4,28},{5,29},{6,30},{7,31},{8,0},{9,1... | collective-permute-start | bytes 1179656 | tf_op jit(solution)/shard_map/ppermute | solution.py:23
  496.9 25.4 %collective-permute-start.24 = (bf16[192,2048]{1,0:T(8,128)(2,1)S(1)}, bf16[192,2048]{1,0:T(8,128)(2,1)S(1)}, u32[]{:S(2)}, u32[]{:S(2)}) collective-permute-start(bf16[192,2048]{1,0:T(8,128)(2,1)S(1)} %get-tuple-element.30), channel_id=1, source_target_pairs={{0,8},{1,9},{2,10},{3,11},{4,12},{5,13},{6,14},{7,15},{8,16},{9,17... | collective-permute-start | bytes 2359304 | tf_op jit(solution)/shard_map/ppermute | solution.py:23
  502.7 16.6 %collective-permute-start.21 = (bf16[96,2048]{1,0:T(8,128)(2,1)S(1)}, bf16[96,2048]{1,0:T(8,128)(2,1)S(1)}, u32[]{:S(2)}, u32[]{:S(2)}) collective-permute-start(bf16[96,2048]{1,0:T(8,128)(2,1)S(1)} %collective-permute-done.20), channel_id=1, source_target_pairs={{0,8},{1,9},{2,10},{3,11},{4,12},{5,13},{6,14},{7,15},{8,16},{9,17... | collective-permute-start | bytes 1179656 | tf_op jit(solution)/shard_map/ppermute | solution.py:23
  512.6 9.7 %collective-permute-start.23 = (bf16[96,2048]{1,0:T(8,128)(2,1)S(1)}, bf16[96,2048]{1,0:T(8,128)(2,1)S(1)}, u32[]{:S(2)}, u32[]{:S(2)}) collective-permute-start(bf16[96,2048]{1,0:T(8,128)(2,1)S(1)} %collective-permute-done.22), channel_id=1, source_target_pairs={{0,24},{1,25},{2,26},{3,27},{4,28},{5,29},{6,30},{7,31},{8,0},{9,1... | collective-permute-start | bytes 1179656 | tf_op jit(solution)/shard_map/ppermute | solution.py:23
  527.6 108.4 %reduce-scatter.11.cloned.1.call-start = ((), (), s32[]{:S(2)}) async-start(), calls=%async_computation.11 | async-start | bytes 2359296 | tf_op jit(solution)/shard_map/reduce_scatter | solution.py:80
  540.1 30.2 %collective-permute-start.44 = (bf16[192,2048]{1,0:T(8,128)(2,1)}, bf16[192,2048]{1,0:T(8,128)(2,1)}, u32[]{:S(2)}, u32[]{:S(2)}) collective-permute-start(bf16[192,2048]{1,0:T(8,128)(2,1)} %get-tuple-element.11), channel_id=1, source_target_pairs={{0,24},{1,25},{2,26},{3,27},{4,28},{5,29},{6,30},{7,31},{8,0},{9,1... | collective-permute-start | bytes 2359304 | tf_op jit(solution)/shard_map/ppermute | solution.py:23
  544.4 15.5 %collective-permute-start.45 = (bf16[96,2048]{1,0:T(8,128)(2,1)S(1)}, bf16[96,2048]{1,0:T(8,128)(2,1)}, u32[]{:S(2)}, u32[]{:S(2)}) collective-permute-start(bf16[96,2048]{1,0:T(8,128)(2,1)S(1)} %get-tuple-element.14), channel_id=1, source_target_pairs={{0,8},{1,9},{2,10},{3,11},{4,12},{5,13},{6,14},{7,15},{8,16},{9,17... | collective-permute-start | bytes 1179656 | tf_op jit(solution)/shard_map/ppermute | solution.py:23
  547.8 18.2 %collective-permute-start.47 = (bf16[96,2048]{1,0:T(8,128)(2,1)}, bf16[96,2048]{1,0:T(8,128)(2,1)}, u32[]{:S(2)}, u32[]{:S(2)}) collective-permute-start(bf16[96,2048]{1,0:T(8,128)(2,1)} %get-tuple-element.13), channel_id=1, source_target_pairs={{0,24},{1,25},{2,26},{3,27},{4,28},{5,29},{6,30},{7,31},{8,0},{9,1... | collective-permute-start | bytes 1179656 | tf_op jit(solution)/shard_map/ppermute | solution.py:23
  551.8 31.1 %collective-permute-start.49 = (bf16[192,2048]{1,0:T(8,128)(2,1)}, bf16[192,2048]{1,0:T(8,128)(2,1)}, u32[]{:S(2)}, u32[]{:S(2)}) collective-permute-start(bf16[192,2048]{1,0:T(8,128)(2,1)} %get-tuple-element.10), channel_id=1, source_target_pairs={{0,8},{1,9},{2,10},{3,11},{4,12},{5,13},{6,14},{7,15},{8,16},{9,17... | collective-permute-start | bytes 2359304 | tf_op jit(solution)/shard_map/ppermute | solution.py:23
  559.9 20.5 %collective-permute-start.46 = (bf16[96,2048]{1,0:T(8,128)(2,1)}, bf16[96,2048]{1,0:T(8,128)(2,1)}, u32[]{:S(2)}, u32[]{:S(2)}) collective-permute-start(bf16[96,2048]{1,0:T(8,128)(2,1)} %collective-permute-done.45), channel_id=1, source_target_pairs={{0,8},{1,9},{2,10},{3,11},{4,12},{5,13},{6,14},{7,15},{8,16},{9,17... | collective-permute-start | bytes 1179656 | tf_op jit(solution)/shard_map/ppermute | solution.py:23
  566.0 16.2 %collective-permute-start.48 = (bf16[96,2048]{1,0:T(8,128)(2,1)}, bf16[96,2048]{1,0:T(8,128)(2,1)S(1)}, u32[]{:S(2)}, u32[]{:S(2)}) collective-permute-start(bf16[96,2048]{1,0:T(8,128)(2,1)} %collective-permute-done.47), channel_id=1, source_target_pairs={{0,24},{1,25},{2,26},{3,27},{4,28},{5,29},{6,30},{7,31},{8,0},{9,1... | collective-permute-start | bytes 1179656 | tf_op jit(solution)/shard_map/ppermute | solution.py:23
  (29 other events, 298.3 us)
Sparse Core Ops, SparseCore 0:
  11.7 48.9 all-gather.8
  63.3 42.6 all-gather.4
  225.5 45.5 reduce-scatter.8
  291.8 44.0 reduce-scatter.4
  345.2 42.5 all-gather.6
  390.3 42.1 all-gather.10
  527.7 44.1 reduce-scatter.6
  592.3 43.7 reduce-scatter.10

commit v2 on v1

v2 whole, which is shorter than its diff:
```python
import functools

import jax
import jax.numpy as jnp
from jax import lax
from jax.experimental import pallas as pl
from jax.experimental.pallas import tpu as pltpu
from jax.sharding import PartitionSpec as P

TICKS = 2
CAP = 24
NX = 4
NZ = 8
RING = 4


def from_behind(block, axis, distance):
    devices = range(lax.axis_size(axis))
    route = [((i - distance) % len(devices), i) for i in devices]
    return lax.ppermute(block, axis, route)


def from_partner(block):
    return lax.ppermute(block, "expert", [(i, i ^ 1) for i in range(NX * NZ)])


def neighbours(axis):
    me = lax.axis_index("expert")
    x, z = me // NZ, me % NZ
    if axis == "x":
        return ((x + 1) % NX) * NZ + z, ((x + NX - 1) % NX) * NZ + z
    return x * NZ + (z + 2) % NZ, x * NZ + (z + NZ - 2) % NZ


def exchange_kernel(jobs, *refs):
    count = len(jobs)
    ins, outs = refs[:count], refs[count : 2 * count]
    relays = refs[2 * count : 3 * count]
    send, recv = refs[3 * count :]
    rings = {axis: neighbours(axis) for axis in dict.fromkeys(axis for axis, _ in jobs)}
    barrier = pltpu.get_barrier_semaphore()
    for pair in rings.values():
        for other in pair:
            pl.semaphore_signal(
                barrier,
                inc=1,
                device_id={"expert": other},
                device_id_type=pl.DeviceIdType.MESH,
            )
    pl.semaphore_wait(barrier, 2 * len(rings))

    def copy(job, number, src, dst, way):
        return pltpu.make_async_remote_copy(
            src_ref=src,
            dst_ref=dst,
            send_sem=send.at[job, number],
            recv_sem=recv.at[job, number],
            device_id={"expert": rings[jobs[job][0]][way]},
            device_id_type=pl.DeviceIdType.MESH,
        )

    first, later, direct = [], [], []
    for job, (_, kind) in enumerate(jobs):
        src, dst, relay = ins[job], outs[job], relays[job]
        rows = dst.shape[1]
        low, high = pl.ds(0, rows // 2), pl.ds(rows // 2, rows // 2)
        if kind == "gather":
            first.append(copy(job, 0, src.at[low], dst.at[1, low], 0))
            first.append(copy(job, 1, src.at[high], dst.at[3, high], 1))
            direct.append(copy(job, 2, src.at[high], dst.at[1, high], 0))
            direct.append(copy(job, 3, src.at[low], dst.at[3, low], 1))
            later.append(copy(job, 4, dst.at[1, low], dst.at[2, low], 0))
            later.append(copy(job, 5, dst.at[3, high], dst.at[2, high], 1))
        else:
            there, back = (0, 1) if kind == "swap" else (1, 0)
            first.append(copy(job, 0, src.at[2, low], relay.at[0], 0))
            first.append(copy(job, 1, src.at[2, high], relay.at[1], 1))
            direct.append(copy(job, 2, src.at[1], dst.at[1], there))
            direct.append(copy(job, 3, src.at[3], dst.at[3], back))
            later.append(copy(job, 4, relay.at[0], dst.at[2, low], 0))
            later.append(copy(job, 5, relay.at[1], dst.at[2, high], 1))
    for one in first + direct:
        one.start()
    for job, (_, kind) in enumerate(jobs):
        outs[job][0] = ins[job][...] if kind == "gather" else ins[job][0]
    for early, late in zip(first, later):
        early.wait_recv()
        late.start()
    for one in first:
        one.wait_send()
    for one in direct + later:
        one.wait()


def exchange(number, jobs, *arrays):
    shapes, relays, sent = [], [], 0
    for (_, kind), array in zip(jobs, arrays):
        rows, width = array.shape[-2:]
        shapes.append(jax.ShapeDtypeStruct((RING, rows, width), array.dtype))
        relays.append(pltpu.VMEM((2, rows // 2, width), array.dtype))
        sent += 4 * rows * width * 2
    whole = pl.BlockSpec(memory_space=pltpu.VMEM)
    return pl.pallas_call(
        functools.partial(exchange_kernel, jobs),
        out_shape=shapes,
        in_specs=[whole] * len(jobs),
        out_specs=[whole] * len(jobs),
        scratch_shapes=relays
        + [pltpu.SemaphoreType.DMA((len(jobs), 6)), pltpu.SemaphoreType.DMA((len(jobs), 6))],
        cost_estimate=pl.CostEstimate(flops=0, bytes_accessed=64_000_000, transcendentals=0),
        compiler_params=pltpu.CompilerParams(collective_id=number, has_side_effects=True),
    )(*arrays)


def normed_rows(hidden, gain_row):
    widened = hidden.astype(jnp.float32)
    scale_inv = lax.rsqrt(jnp.mean(widened * widened, axis=-1, keepdims=True) + 1e-06)
    return (widened * scale_inv * gain_row).astype(jnp.bfloat16)


def routing(ids, weights, x_index, half):
    tok = ids.shape[-1]
    wanted = 2 * ((x_index + jnp.arange(NX, dtype=jnp.int32)) % NX) + half
    match = ids[None] == wanted[:, None, None, None]
    weight = jnp.sum(jnp.where(match, weights[None], 0.0), axis=2)
    chosen = jnp.any(match, axis=2)
    count = chosen.astype(jnp.int32)
    rank = jnp.cumsum(count, axis=-1) - count
    slot = jnp.arange(CAP, dtype=jnp.int32)
    hot = chosen[:, :, None, :] & (rank[:, :, None, :] == slot[None, None, :, None])
    same = jnp.eye(RING, dtype=jnp.bool_)
    block = hot[:, :, :, None, :] & same[None, :, None, :, None]
    pick = block.astype(jnp.bfloat16).reshape(NX * RING * CAP, RING * tok)
    high = lax.reduce_precision(weight, 8, 7)
    low = weight - high
    parts = []
    for part in (high, low):
        spread = jnp.where(block, part[:, :, None, None, :], 0.0).astype(jnp.bfloat16)
        parts.append(spread.reshape(NX * RING * CAP, RING * tok))
    return pick, parts


def picked(plan, normed):
    width = normed.shape[-1]
    rows = jnp.dot(plan[0], normed.reshape(-1, width), preferred_element_type=jnp.float32)
    return rows.astype(jnp.bfloat16).reshape(RING, -1, width)


def expert_rows(rows, gate_local, up_local, down_local):
    blocks, count, width = rows.shape
    rows = rows.reshape(-1, width)
    gate_act = jnp.dot(rows, gate_local, preferred_element_type=jnp.float32)
    up_act = jnp.dot(rows, up_local, preferred_element_type=jnp.float32)
    activated = (jax.nn.silu(gate_act) * up_act).astype(jnp.bfloat16)
    out = jnp.dot(activated, down_local, preferred_element_type=jnp.float32)
    return out.astype(jnp.bfloat16).reshape(blocks, count, width)


def combined(plan, back):
    width = back.shape[-1]
    back = back.reshape(-1, width)
    dims = (((0,), (0,)), ((), ()))
    moe = sum(
        lax.dot_general(part, back, dims, preferred_element_type=jnp.float32) for part in plan[1]
    )
    return moe.astype(jnp.bfloat16).reshape(RING, -1, width)


def finished(hidden, partial):
    moe = jnp.sum(partial.astype(jnp.float32), axis=0)
    return (hidden.astype(jnp.float32) + moe).astype(jnp.bfloat16)


X_THERE = (("x", "swap"),)
X_BACK = (("x", "back"),)
Z_BACK = (("z", "back"),)
START = (("z", "gather"), ("z", "gather"))
GATHER = (("x", "back"), ("z", "gather"))
RETURN = (("x", "swap"), ("z", "back"))


def body(
    fwd_state,
    rev_state,
    norm_gain,
    gate_weight,
    up_weight,
    down_weight,
    fwd_routes,
    rev_routes,
    fwd_combine,
    rev_combine,
):
    index = lax.axis_index("expert")
    x_index = index // NZ
    half = (index % NZ) // (NZ // 2)
    gain_row = norm_gain[0]
    gate, up, down = gate_weight[0], up_weight[0], down_weight[0]
    weights = (
        jnp.concatenate([gate, from_partner(gate)], axis=1),
        jnp.concatenate([up, from_partner(up)], axis=1),
        jnp.concatenate([down, from_partner(down)], axis=0),
    )
    tok = fwd_state.shape[1]
    tables = [a[:, 0].astype(jnp.float32) for a in (fwd_routes, rev_routes, fwd_combine, rev_combine)]
    table = jnp.stack(tables).transpose(0, 1, 3, 2).reshape(-1, tok)
    table = jnp.pad(table, ((0, 0), (0, 128 - tok)))
    fwd, rev = fwd_state[0], rev_state[0]
    fwd_rows, table = exchange(1, START, normed_rows(fwd, gain_row), table)
    table = table[:, :, :tok].reshape(RING, 4, TICKS, 2, tok)

    def plan(stream, tick):
        ids = table[:, stream, tick].astype(jnp.int32)
        return routing(ids, table[:, 2 + stream, tick], x_index, half)

    fwd_plan, rev_plan = plan(0, 0), plan(1, 0)
    (fwd_rows,) = exchange(2, X_THERE, picked(fwd_plan, fwd_rows))
    for tick in range(TICKS):
        fwd_rows, rev_rows = exchange(
            3, GATHER, expert_rows(fwd_rows, *weights), normed_rows(rev, gain_row)
        )
        rev_rows, fwd_rows = exchange(
            4, RETURN, picked(rev_plan, rev_rows), combined(fwd_plan, fwd_rows)
        )
        fwd = finished(fwd, fwd_rows)
        if tick + 1 < TICKS:
            fwd = from_behind(fwd, "pipe", 1)
            fwd_plan = plan(0, tick + 1)
            rev_rows, fwd_rows = exchange(
                3, GATHER, expert_rows(rev_rows, *weights), normed_rows(fwd, gain_row)
            )
            fwd_rows, rev_rows = exchange(
                4, RETURN, picked(fwd_plan, fwd_rows), combined(rev_plan, rev_rows)
            )
            rev = from_behind(finished(rev, rev_rows), "pipe", -1)
            rev_plan = plan(1, tick + 1)
        else:
            (rev_rows,) = exchange(6, X_BACK, expert_rows(rev_rows, *weights))
            (rev_rows,) = exchange(5, Z_BACK, combined(rev_plan, rev_rows))
            rev = finished(rev, rev_rows)
    return (fwd[None], rev[None])


def solution(mesh):
    placed = (
        P("pipe", "expert", None),
        P("pipe", "expert", None),
        P("pipe", None),
        P("pipe", None, "expert"),
        P("pipe", None, "expert"),
        P("pipe", "expert", None),
        P(None, "pipe", "expert", None),
        P(None, "pipe", "expert", None),
        P(None, "pipe", "expert", None),
        P(None, "pipe", "expert", None),
    )
    return jax.shard_map(
        body,
        mesh=mesh,
        in_specs=placed,
        out_specs=(P("pipe", "expert", None), P("pipe", "expert", None)),
        check_vma=False,
    )
```

time: 656 us -> 404 us (0.62)
  the two profiles are of different devices: /device:TPU:2 before, /device:TPU:8 now
where the time goes in v2:
time: 404 us; the launch traced here: 403 us
  Pallas kernels  303 us (75%)
  matrix products  54.3 us (13%)
  other arithmetic  23.7 us (6%)
  starting transfers between devices  10.6 us (3%)
  local copies, waits for them, and re-layouts  10 us (2%)
    pallas_call x10, Pallas kernels, exchange(): pl.pallas_call(functools.partial(exchange_kernel, jobs), out_shape=shapes...  303 us
    dot_general x4, matrix products, expert_rows(): out = jnp.dot(activated, down_local, preferred_element_type=jnp.float32)  20.6 us
    dot_general x4, matrix products, expert_rows(): gate_act = jnp.dot(rows, gate_local, preferred_element_type=jnp.float32)  11.5 us
    dot_general x8, matrix products, combined(): lax.dot_general(part, back, dims, preferred_element_type=jnp.float32)  11.3 us
    dot_general x4, matrix products, picked(): jnp.dot(plan[0], normed.reshape(-1, width), preferred_element_type=jnp.fl...  11 us
    ppermute x3, starting transfers between devices, from_partner(): return lax.ppermute(block, 'expert', [(i, i ^ 1) for i in range(NX * NZ)])  10.1 us
  transfers between devices with their start and end apart: 5, of which 0 were waited for; matrix products, arithmetic and copies ran while one was open for 11% of the time, Pallas kernels for 22%

profile of v2, /device:TPU:8, one launch (start us, length us, event | category | flops | bytes accessed | tf_op | source)
XLA Modules:
  0.0 403.1 jit_solution(16709995048012814824)
XLA Ops:
  0.6 4.3 %collective-permute-start = (bf16[2048,192]{0,1:T(8,128)(2,1)}, bf16[2048,192]{0,1:T(8,128)(2,1)}, u32[]{:S(2)}, u32[]{:S(2)}) collective-permute-start(bf16[2048,192]{0,1:T(8,128)(2,1)} %bitcast.172), channel_id=1, source_target_pairs={{0,1},{1,0},{2,3},{3,2},{4,5},{5,4},{6,7},{7,6},{8,9},{9,8},{10,11... | collective-permute-start | bytes 2359304 | tf_op jit(solution)/shard_map/ppermute | solution.py:24
  4.9 1.9 collective-permute-start.1
  6.9 3.9 collective-permute-start.2
  10.9 1.1 fusion.12
  12.0 1.1 fusion.16
  13.1 0.7 fusion.38
  13.8 0.7 pad_maximum_fusion.3
  14.5 0.6 pad.4.refs_1_
  15.1 2.0 fusion.18
  17.1 65.7 %shard_map.113 = (bf16[4,64,2048]{2,1,0:T(8,128)(2,1)}, f32[4,16,128]{2,1,0:T(8,128)}) custom-call(bf16[64,2048]{1,0:T(8,128)(2,1)} %get-tuple-element.63.refs_0_, f32[16,128]{1,0:T(8,128)} %pad.4.refs_1_), custom_call_target="tpu_custom_call" | custom-call | bytes 64000000 | tf_op jit(solution)/shard_map/pallas_call | solution.py:103
  82.8 0.8 slice_bitcast_fusion.2
  84.0 1.0 reduce_window_sum.23
  84.9 0.9 reduce_window_sum.27
  85.9 0.9 reduce_window_sum.32
  86.8 0.9 reduce_window_sum.22
  88.1 0.4 copy-done.12
  88.5 1.1 broadcast_and_fusion.2
  89.7 0.4 and.248
  90.0 1.0 and.253
  91.0 1.0 and.258
  92.0 1.0 and.243
  93.1 1.7 convolution_convert_fusion.7
  94.8 23.5 %shard_map.114 = bf16[4,96,2048]{2,1,0:T(8,128)(2,1)} custom-call(bf16[4,96,2048]{2,1,0:T(8,128)(2,1)} %bitcast.126), custom_call_target="tpu_custom_call" | custom-call | bytes 64000000 | tf_op jit(solution)/shard_map/pallas_call | solution.py:103
  118.4 2.2 select_convert_fusion
  120.5 0.9 convert_element_type.388
  121.5 0.9 convert_element_type.384
  122.4 1.0 convert_element_type.377
  123.4 1.0 convert_element_type.379
  125.5 3.2 fusion.54
  128.7 5.1 %convolution_convert_fusion.3 = bf16[384,2048]{1,0:T(8,128)(2,1)} fusion(f32[384,384]{1,0:T(8,128)} %fusion.54, bf16[192,2048]{1,0:T(8,128)(2,1)} %collective-permute-done.2, bf16[192,2048]{1,0:T(8,128)(2,1)} %bitcast.178, bf16[384,2048]{1,0:T(8,128)(2,1)S(1)} %bitcast.138, bf16[2048,192]{0,1:T(8,128)(2,1)} %collective-permute-done.1, ...), kind=kOutput, calls=%fused_computation.3 | convolution fusion | flops 1215922176 | bytes 6881280 | tf_op jit(solution)/shard_map/dot_general | solution.py:155
  133.8 22.6 %shard_map.115 = (bf16[4,96,2048]{2,1,0:T(8,128)(2,1)}, bf16[4,64,2048]{2,1,0:T(8,128)(2,1)}) custom-call(bf16[4,96,2048]{2,1,0:T(8,128)(2,1)} %bitcast.141, bf16[64,2048]{1,0:T(8,128)(2,1)} %get-tuple-element.62.refs_1_), custom_call_target="tpu_custom_call" | custom-call | bytes 64000000 | tf_op jit(solution)/shard_map/pallas_call | solution.py:103
  156.4 3.1 convolution_convert_fusion.6
  159.5 0.7 fusion.55
  160.2 1.7 fusion
  161.9 24.8 %shard_map.116 = (bf16[4,96,2048]{2,1,0:T(8,128)(2,1)}, bf16[4,64,2048]{2,1,0:T(8,128)(2,1)}) custom-call(bf16[4,96,2048]{2,1,0:T(8,128)(2,1)} %bitcast.123, bf16[4,64,2048]{2,1,0:T(8,128)(2,1)} %bitcast.133), custom_call_target="tpu_custom_call" | custom-call | bytes 64000000 | tf_op jit(solution)/shard_map/pallas_call | solution.py:103
  186.7 1.6 convert_reduce_fusion.3
  188.6 3.2 fusion.53
  191.8 5.3 %convolution_convert_fusion.2 = bf16[384,2048]{1,0:T(8,128)(2,1)} fusion(f32[384,384]{1,0:T(8,128)} %fusion.53, bf16[192,2048]{1,0:T(8,128)(2,1)} %collective-permute-done.2, bf16[192,2048]{1,0:T(8,128)(2,1)S(1)} %bitcast.180, bf16[384,2048]{1,0:T(8,128)(2,1)} %bitcast.166, bf16[2048,192]{0,1:T(8,128)(2,1)} %collective-permute-done.1, ...), kind=kOutput, calls=%fused_computation.2 | convolution fusion | flops 1215922176 | bytes 6881280 | tf_op jit(solution)/shard_map/dot_general | solution.py:155
  197.3 0.8 fusion.6.refs_1_
  198.2 27.1 %shard_map.117 = (bf16[4,96,2048]{2,1,0:T(8,128)(2,1)}, bf16[4,64,2048]{2,1,0:T(8,128)(2,1)}) custom-call(bf16[4,96,2048]{2,1,0:T(8,128)(2,1)} %bitcast.139, bf16[64,2048]{1,0:T(8,128)(2,1)} %fusion.6.refs_1_), custom_call_target="tpu_custom_call" | custom-call | bytes 64000000 | tf_op jit(solution)/shard_map/pallas_call | solution.py:103
  225.3 3.1 convolution_convert_fusion.5
  228.4 0.7 fusion.56
  229.1 1.7 fusion.1
  230.8 29.5 %shard_map.118 = (bf16[4,96,2048]{2,1,0:T(8,128)(2,1)}, bf16[4,64,2048]{2,1,0:T(8,128)(2,1)}) custom-call(bf16[4,96,2048]{2,1,0:T(8,128)(2,1)} %bitcast.124, bf16[4,64,2048]{2,1,0:T(8,128)(2,1)} %bitcast.134), custom_call_target="tpu_custom_call" | custom-call | bytes 64000000 | tf_op jit(solution)/shard_map/pallas_call | solution.py:103
  260.4 1.5 convert_reduce_fusion.2
  262.0 0.4 collective-permute-start.4
  262.4 2.1 fusion.52
  264.5 5.1 %convolution_convert_fusion.1 = bf16[384,2048]{1,0:T(8,128)(2,1)} fusion(f32[384,384]{1,0:T(8,128)S(1)} %fusion.52, bf16[192,2048]{1,0:T(8,128)(2,1)} %collective-permute-done.2, bf16[192,2048]{1,0:T(8,128)(2,1)S(1)} %bitcast.181, bf16[384,2048]{1,0:T(8,128)(2,1)} %bitcast.168, bf16[2048,192]{0,1:T(8,128)(2,1)} %collective-permute-done.1, ...), kind=kOutput, calls=%fused_computation.1 | convolution fusion | flops 1215922176 | bytes 6881280 | tf_op jit(solution)/shard_map/dot_general | solution.py:155
  269.8 0.8 fusion.10.refs_1_
  270.7 27.7 %shard_map.119 = (bf16[4,96,2048]{2,1,0:T(8,128)(2,1)}, bf16[4,64,2048]{2,1,0:T(8,128)(2,1)}) custom-call(bf16[4,96,2048]{2,1,0:T(8,128)(2,1)} %bitcast.140, bf16[64,2048]{1,0:T(8,128)(2,1)} %fusion.10.refs_1_), custom_call_target="tpu_custom_call" | custom-call | bytes 64000000 | tf_op jit(solution)/shard_map/pallas_call | solution.py:103
  298.4 3.1 convolution_convert_fusion.4
  301.5 0.7 fusion.57
  302.4 1.7 fusion.2
  304.1 31.1 %shard_map.120 = (bf16[4,96,2048]{2,1,0:T(8,128)(2,1)}, bf16[4,64,2048]{2,1,0:T(8,128)(2,1)}) custom-call(bf16[4,96,2048]{2,1,0:T(8,128)(2,1)} %bitcast.125, bf16[4,64,2048]{2,1,0:T(8,128)(2,1)} %bitcast.135), custom_call_target="tpu_custom_call" | custom-call | bytes 64000000 | tf_op jit(solution)/shard_map/pallas_call | solution.py:103
  335.2 1.5 convert_reduce_fusion.1
  336.9 2.9 fusion.51
  339.9 5.1 %convolution_convert_fusion = bf16[384,2048]{1,0:T(8,128)(2,1)} fusion(f32[384,384]{1,0:T(8,128)} %fusion.51, bf16[192,2048]{1,0:T(8,128)(2,1)} %collective-permute-done.2, bf16[192,2048]{1,0:T(8,128)(2,1)} %bitcast.179, bf16[384,2048]{1,0:T(8,128)(2,1)S(1)} %bitcast.171, bf16[2048,192]{0,1:T(8,128)(2,1)} %collective-permute-done.1, ...), kind=kOutput, calls=%fused_computation | convolution fusion | flops 1215922176 | bytes 6881280 | tf_op jit(solution)/shard_map/dot_general | solution.py:155
  344.9 21.8 %shard_map.121 = bf16[4,96,2048]{2,1,0:T(8,128)(2,1)} custom-call(bf16[4,96,2048]{2,1,0:T(8,128)(2,1)} %bitcast.142), custom_call_target="tpu_custom_call" | custom-call | bytes 64000000 | tf_op jit(solution)/shard_map/pallas_call | solution.py:103
  366.8 2.3 fusion.58
  369.1 1.7 fusion.3
  370.8 29.3 %shard_map.122 = bf16[4,64,2048]{2,1,0:T(8,128)(2,1)} custom-call(bf16[4,64,2048]{2,1,0:T(8,128)(2,1)} %bitcast.136), custom_call_target="tpu_custom_call" | custom-call | bytes 64000000 | tf_op jit(solution)/shard_map/pallas_call | solution.py:103
  400.1 1.4 convert_reduce_fusion
  401.5 0.8 fusion.25
  402.3 0.8 fusion.24
  (106 shorter events, 2.7 us)
Async XLA Ops:
  0.6 124.8 %collective-permute-start = (bf16[2048,192]{0,1:T(8,128)(2,1)}, bf16[2048,192]{0,1:T(8,128)(2,1)}, u32[]{:S(2)}, u32[]{:S(2)}) collective-permute-start(bf16[2048,192]{0,1:T(8,128)(2,1)} %bitcast.172), channel_id=1, source_target_pairs={{0,1},{1,0},{2,3},{3,2},{4,5},{5,4},{6,7},{7,6},{8,9},{9,8},{10,11... | collective-permute-start | bytes 2359304 | tf_op jit(solution)/shard_map/ppermute | solution.py:24
  4.9 123.8 %collective-permute-start.1 = (bf16[2048,192]{0,1:T(8,128)(2,1)}, bf16[2048,192]{0,1:T(8,128)(2,1)}, u32[]{:S(2)}, u32[]{:S(2)}) collective-permute-start(bf16[2048,192]{0,1:T(8,128)(2,1)} %bitcast.182), channel_id=1, source_target_pairs={{0,1},{1,0},{2,3},{3,2},{4,5},{5,4},{6,7},{7,6},{8,9},{9,8},{10,11... | collective-permute-start | bytes 2359304 | tf_op jit(solution)/shard_map/ppermute | solution.py:24
  6.9 121.8 %collective-permute-start.2 = (bf16[192,2048]{1,0:T(8,128)(2,1)}, bf16[192,2048]{1,0:T(8,128)(2,1)}, u32[]{:S(2)}, u32[]{:S(2)}) collective-permute-start(bf16[192,2048]{1,0:T(8,128)(2,1)} %bitcast.177), channel_id=1, source_target_pairs={{0,1},{1,0},{2,3},{3,2},{4,5},{5,4},{6,7},{7,6},{8,9},{9,8},{10,11... | collective-permute-start | bytes 2359304 | tf_op jit(solution)/shard_map/ppermute | solution.py:24
  10.8 78.8 %copy-start.24 = (pred[4,4]{1,0:T(4,128)(4,1)}, pred[4,4]{1,0:T(4,128)(4,1)S(1)}, u32[]{:S(2)}) copy-start(pred[4,4]{1,0:T(4,128)(4,1)S(1)} %iota_compare_fusion.4) | copy-start | bytes 52
  82.8 10.3 %copy-start.7 = (bf16[4,64,2048]{2,1,0:T(8,128)(2,1)S(1)}, bf16[4,64,2048]{2,1,0:T(8,128)(2,1)}, u32[]{:S(2)}) copy-start(bf16[4,64,2048]{2,1,0:T(8,128)(2,1)} %get-tuple-element.17) | copy-start | bytes 3145732
  87.8 0.6 copy-start.12
  87.9 1.7 copy-start.14
  88.0 1.6 copy-start.16
  88.5 1.2 copy-start.18
  94.8 23.5 %copy-start.13 = (pred[4,4,24,64]{3,2,1,0:T(8,128)(4,1)S(1)}, pred[4,4,24,64]{3,2,1,0:T(8,128)(4,1)}, u32[]{:S(2)}) copy-start(pred[4,4,24,64]{3,2,1,0:T(8,128)(4,1)} %copy-done.12) | copy-start | bytes 73732
  94.8 23.5 %copy-start.15 = (pred[4,4,24,64]{3,2,1,0:T(8,128)(4,1)S(1)}, pred[4,4,24,64]{3,2,1,0:T(8,128)(4,1)}, u32[]{:S(2)}) copy-start(pred[4,4,24,64]{3,2,1,0:T(8,128)(4,1)} %copy-done.14) | copy-start | bytes 73732
  94.8 23.5 %copy-start.17 = (pred[4,4,24,64]{3,2,1,0:T(8,128)(4,1)S(1)}, pred[4,4,24,64]{3,2,1,0:T(8,128)(4,1)}, u32[]{:S(2)}) copy-start(pred[4,4,24,64]{3,2,1,0:T(8,128)(4,1)} %copy-done.16) | copy-start | bytes 73732
  94.8 23.5 %copy-start.19 = (pred[4,4,24,64]{3,2,1,0:T(8,128)(4,1)S(1)}, pred[4,4,24,64]{3,2,1,0:T(8,128)(4,1)}, u32[]{:S(2)}) copy-start(pred[4,4,24,64]{3,2,1,0:T(8,128)(4,1)} %copy-done.18) | copy-start | bytes 73732
  94.8 23.6 %copy-start.25 = (pred[4,4]{1,0:T(4,128)(4,1)S(1)}, pred[4,4]{1,0:T(4,128)(4,1)}, u32[]{:S(2)}) copy-start(pred[4,4]{1,0:T(4,128)(4,1)} %copy-done.24) | copy-start | bytes 52
  123.4 2.1 copy-start.6
  133.7 22.6 %copy-start.22 = (pred[384,256]{1,0:T(32,128)(4,1)S(1)}, pred[384,256]{1,0:T(32,128)(4,1)}, u32[]{:S(2)}) copy-start(pred[384,256]{1,0:T(32,128)(4,1)} %and.243) | copy-start | bytes 294916
  156.4 3.1 copy-start.1
  161.9 26.4 %copy-start.4 = (bf16[1,64,2048]{2,1,0:T(8,128)(2,1)S(1)}, bf16[1,64,2048]{2,1,0:T(8,128)(2,1)}, u32[]{:S(2)}) copy-start(bf16[1,64,2048]{2,1,0:T(8,128)(2,1)} %param.10) | copy-start | bytes 786436
  186.7 1.7 copy-start.26
  186.7 1.9 copy-start.29
  188.4 8.8 %collective-permute-start.3 = (bf16[64,2048]{1,0:T(8,128)(2,1)S(1)}, bf16[64,2048]{1,0:T(8,128)(2,1)S(1)}, u32[]{:S(2)}, u32[]{:S(2)}) collective-permute-start(bf16[64,2048]{1,0:T(8,128)(2,1)S(1)} %fusion.15), channel_id=1, source_target_pairs={{480,0},{0,32},{32,64},{64,96},{96,128},{128,160},{160,192},{192,2... | collective-permute-start | bytes 786440 | tf_op jit(solution)/shard_map/ppermute | solution.py:20
  188.6 3.2 copy-start.30
  191.8 5.5 %copy-start.23 = (f32[1,2048]{1,0:T(1,128)S(1)}, f32[1,2048]{1,0:T(1,128)}, u32[]{:S(2)}) copy-start(f32[1,2048]{1,0:T(1,128)} %param.12) | copy-start | bytes 24580
  197.2 28.1 %copy-start.21 = (pred[384,256]{1,0:T(32,128)(4,1)S(1)}, pred[384,256]{1,0:T(32,128)(4,1)}, u32[]{:S(2)}) copy-start(pred[384,256]{1,0:T(32,128)(4,1)} %and.258) | copy-start | bytes 294916
  225.3 3.1 copy-start.2
  230.8 31.1 %copy-start.5 = (bf16[1,64,2048]{2,1,0:T(8,128)(2,1)S(1)}, bf16[1,64,2048]{2,1,0:T(8,128)(2,1)}, u32[]{:S(2)}) copy-start(bf16[1,64,2048]{2,1,0:T(8,128)(2,1)} %param.11) | copy-start | bytes 786436
  260.4 2.0 copy-start.27
  262.0 7.7 %collective-permute-start.4 = (bf16[64,2048]{1,0:T(8,128)(2,1)S(1)}, bf16[64,2048]{1,0:T(8,128)(2,1)S(1)}, u32[]{:S(2)}, u32[]{:S(2)}) collective-permute-start(bf16[64,2048]{1,0:T(8,128)(2,1)S(1)} %fusion.19), channel_id=1, source_target_pairs={{32,0},{64,32},{96,64},{128,96},{160,128},{192,160},{224,192},{256... | collective-permute-start | bytes 786440 | tf_op jit(solution)/shard_map/ppermute | solution.py:20
  269.6 28.7 %copy-start.20 = (pred[384,256]{1,0:T(32,128)(4,1)S(1)}, pred[384,256]{1,0:T(32,128)(4,1)}, u32[]{:S(2)}) copy-start(pred[384,256]{1,0:T(32,128)(4,1)} %and.253) | copy-start | bytes 294916
  298.3 3.1 copy-start.3
  298.3 3.1 copy-start.11
  301.5 0.9 copy-start.9
  335.2 1.7 copy-start.28
  344.9 21.8 %copy-start.10 = (bf16[384,256]{1,0:T(8,128)(2,1)S(1)}, bf16[384,256]{1,0:T(8,128)(2,1)}, u32[]{:S(2)}) copy-start(bf16[384,256]{1,0:T(8,128)(2,1)} %convert_element_type.384) | copy-start | bytes 589828
  366.8 2.3 copy-start
  366.8 2.3 copy-start.8

commit v3 on v2

--- a/solution.py
+++ b/solution.py
@@ -146,13 +146,14 @@
     return rows.astype(jnp.bfloat16).reshape(RING, -1, width)
 
 
-def expert_rows(rows, gate_local, up_local, down_local):
+def expert_rows(rows, gate_up, down):
     blocks, count, width = rows.shape
     rows = rows.reshape(-1, width)
-    gate_act = jnp.dot(rows, gate_local, preferred_element_type=jnp.float32)
-    up_act = jnp.dot(rows, up_local, preferred_element_type=jnp.float32)
-    activated = (jax.nn.silu(gate_act) * up_act).astype(jnp.bfloat16)
-    out = jnp.dot(activated, down_local, preferred_element_type=jnp.float32)
+    dims = (((1,), (1,)), ((), ()))
+    hidden = lax.dot_general(rows, gate_up, dims, preferred_element_type=jnp.float32)
+    units = down.shape[0]
+    activated = (jax.nn.silu(hidden[:, :units]) * hidden[:, units:]).astype(jnp.bfloat16)
+    out = jnp.dot(activated, down, preferred_element_type=jnp.float32)
     return out.astype(jnp.bfloat16).reshape(blocks, count, width)
 
 
@@ -195,18 +196,19 @@
     x_index = index // NZ
     half = (index % NZ) // (NZ // 2)
     gain_row = norm_gain[0]
-    gate, up, down = gate_weight[0], up_weight[0], down_weight[0]
-    weights = (
-        jnp.concatenate([gate, from_partner(gate)], axis=1),
-        jnp.concatenate([up, from_partner(up)], axis=1),
-        jnp.concatenate([down, from_partner(down)], axis=0),
-    )
     tok = fwd_state.shape[1]
     tables = [a[:, 0].astype(jnp.float32) for a in (fwd_routes, rev_routes, fwd_combine, rev_combine)]
     table = jnp.stack(tables).transpose(0, 1, 3, 2).reshape(-1, tok)
     table = jnp.pad(table, ((0, 0), (0, 128 - tok)))
     fwd, rev = fwd_state[0], rev_state[0]
     fwd_rows, table = exchange(1, START, normed_rows(fwd, gain_row), table)
+    mine = jnp.concatenate([gate_weight[0].T, up_weight[0].T, down_weight[0]])
+    mine, fwd_rows, table = lax.optimization_barrier((mine, fwd_rows, table))
+    part = mine.shape[0] // 3
+    other = from_partner(mine)
+    both = jnp.stack([mine.reshape(3, part, -1), other.reshape(3, part, -1)], axis=1)
+    weights = lax.optimization_barrier(both.reshape(3, 2 * part, -1))
+    weights = (weights[:2].reshape(4 * part, -1), weights[2])
     table = table[:, :, :tok].reshape(RING, 4, TICKS, 2, tok)
 
     def plan(stream, tick):

time: 404 us -> 381 us (0.943)
  the two profiles are of different devices: /device:TPU:8 before, /device:TPU:40 now
where the time goes in v3:
time: 381 us; the launch traced here: 379 us
  Pallas kernels  269 us (71%)
  matrix products  47.8 us (13%)
  other arithmetic  27.9 us (7%)
  local copies, waits for them, and re-layouts  23.6 us (6%)
  starting transfers between devices  7.06 us (2%)
    pallas_call x10, Pallas kernels, exchange(): pl.pallas_call(functools.partial(exchange_kernel, jobs), out_shape=shapes...  269 us
    dot_general x4, matrix products, expert_rows(): out = jnp.dot(activated, down, preferred_element_type=jnp.float32)  13.1 us
    dot_general x4, matrix products, expert_rows(): lax.dot_general(rows, gate_up, dims, preferred_element_type=jnp.float32)  11.9 us
    convert_element_type x8, local copies, waits for them, and re-layouts, routing(): jnp.where(block, part[:, :, None, None, :], 0.0).astype(jnp.bfloat16)  11.5 us
    dot_general x8, matrix products, combined(): lax.dot_general(part, back, dims, preferred_element_type=jnp.float32)  11.5 us
    dot_general x4, matrix products, picked(): jnp.dot(plan[0], normed.reshape(-1, width), preferred_element_type=jnp.fl...  11.2 us
  transfers between devices with their start and end apart: 3, of which 2 were waited for; matrix products, arithmetic and copies ran while one was open for 10% of the time, Pallas kernels for 6%

profile of v3, /device:TPU:40, one launch (start us, length us, event | category | flops | bytes accessed | tf_op | source)
XLA Modules:
  0.0 379.3 jit_solution(10473673881226918931)
XLA Ops:
  0.6 1.2 fusion.16
  1.8 1.1 fusion.20
  2.9 0.7 fusion.46
  3.7 0.7 pad_maximum_fusion.2
  5.0 2.0 fusion.22
  7.0 27.6 %shard_map.113 = (bf16[4,64,2048]{2,1,0:T(8,128)(2,1)}, f32[4,16,128]{2,1,0:T(8,128)}) custom-call(bf16[64,2048]{1,0:T(8,128)(2,1)} %get-tuple-element.69.refs_0_, f32[16,128]{1,0:T(8,128)} %pad.4.refs_1_), custom_call_target="tpu_custom_call" | custom-call | bytes 64000000 | tf_op jit(solution)/shard_map/pallas_call | solution.py:103
  34.6 1.6 pad_maximum_fusion.1
  36.2 7.0 %collective-permute-start = (bf16[576,2048]{1,0:T(8,128)(2,1)S(1)}, bf16[576,2048]{1,0:T(8,128)(2,1)}, u32[]{:S(2)}, u32[]{:S(2)}) collective-permute-start(bf16[576,2048]{1,0:T(8,128)(2,1)S(1)} %pad_maximum_fusion.1), channel_id=1, source_target_pairs={{0,1},{1,0},{2,3},{3,2},{4,5},{5,4},{6,7},{7,6},{8,9},{9,8},{10,11... | collective-permute-start | bytes 7077896 | tf_op jit(solution)/shard_map/ppermute | solution.py:24
  43.6 1.0 reduce_window_sum.23
  44.5 0.9 reduce_window_sum.27
  45.5 0.9 reduce_window_sum.32
  46.4 0.9 reduce_window_sum.22
  48.1 1.8 broadcast_and_fusion.2
  49.9 1.3 and.248
  51.2 1.9 and.253
  53.1 1.9 and.258
  55.0 1.9 and.243
  56.9 1.7 convolution_convert_fusion.7
  58.6 24.2 %shard_map.114 = bf16[4,96,2048]{2,1,0:T(8,128)(2,1)} custom-call(bf16[4,96,2048]{2,1,0:T(8,128)(2,1)} %bitcast.146), custom_call_target="tpu_custom_call" | custom-call | bytes 64000000 | tf_op jit(solution)/shard_map/pallas_call | solution.py:103
  83.0 4.1 %select_convert_fusion = (bf16[4,4,24,4,64]{4,3,2,1,0:T(4,128)(2,1)}, bf16[4,4,24,4,64]{4,3,2,1,0:T(4,128)(2,1)}, bf16[4,4,24,4,64]{4,3,2,1,0:T(4,128)(2,1)}, bf...) fusion(bf16[4,4,64]{2,1,0:T(4,128)(2,1)S(1)} %get-tuple-element, ...), kind=kLoop, calls=%fused_computation.29 | loop fusion | flops 1179648 | bytes 1687568 | tf_op jit(solution)/shard_map/convert_element_type | solution.py:138
  87.1 2.0 convert_element_type.388
  89.1 2.0 convert_element_type.384
  91.1 2.0 convert_element_type.377
  93.1 2.0 convert_element_type.379
  95.1 2.0 convert_element_type.347
  97.1 1.0 convert_element_type.349
  98.6 2.1 pad_maximum_fusion
  101.0 2.3 copy-done.8
  103.3 1.4 fusion.55
  104.7 2.3 convolution_convert_fusion.3
  107.0 24.6 %shard_map.115 = (bf16[4,96,2048]{2,1,0:T(8,128)(2,1)}, bf16[4,64,2048]{2,1,0:T(8,128)(2,1)}) custom-call(bf16[4,96,2048]{2,1,0:T(8,128)(2,1)} %bitcast.164, bf16[64,2048]{1,0:T(8,128)(2,1)} %get-tuple-element.68.refs_1_), custom_call_target="tpu_custom_call" | custom-call | bytes 64000000 | tf_op jit(solution)/shard_map/pallas_call | solution.py:103
  131.6 3.2 convolution_convert_fusion.6
  134.8 0.7 fusion.56
  135.7 1.9 fusion
  137.6 30.3 %shard_map.116 = (bf16[4,96,2048]{2,1,0:T(8,128)(2,1)}, bf16[4,64,2048]{2,1,0:T(8,128)(2,1)}) custom-call(bf16[4,96,2048]{2,1,0:T(8,128)(2,1)} %bitcast.143, bf16[4,64,2048]{2,1,0:T(8,128)(2,1)} %bitcast.153), custom_call_target="tpu_custom_call" | custom-call | bytes 64000000 | tf_op jit(solution)/shard_map/pallas_call | solution.py:103
  167.9 1.5 convert_reduce_fusion.3
  169.7 3.3 fusion.57
  173.0 3.6 convolution_convert_fusion.2
  176.7 2.1 collective-permute-done.1
  179.0 0.8 fusion.10.refs_1_
  179.8 23.1 %shard_map.117 = (bf16[4,96,2048]{2,1,0:T(8,128)(2,1)}, bf16[4,64,2048]{2,1,0:T(8,128)(2,1)}) custom-call(bf16[4,96,2048]{2,1,0:T(8,128)(2,1)} %bitcast.162, bf16[64,2048]{1,0:T(8,128)(2,1)} %fusion.10.refs_1_), custom_call_target="tpu_custom_call" | custom-call | bytes 64000000 | tf_op jit(solution)/shard_map/pallas_call | solution.py:103
  203.0 3.2 convolution_convert_fusion.5
  206.1 0.7 fusion.58
  206.9 1.7 fusion.1
  208.6 25.7 %shard_map.118 = (bf16[4,96,2048]{2,1,0:T(8,128)(2,1)}, bf16[4,64,2048]{2,1,0:T(8,128)(2,1)}) custom-call(bf16[4,96,2048]{2,1,0:T(8,128)(2,1)} %bitcast.144, bf16[4,64,2048]{2,1,0:T(8,128)(2,1)} %bitcast.154), custom_call_target="tpu_custom_call" | custom-call | bytes 64000000 | tf_op jit(solution)/shard_map/pallas_call | solution.py:103
  234.3 3.9 %fusion.59 = f32[384,768]{1,0:T(8,128)S(1)} fusion(bf16[384,2048]{1,0:T(8,128)(2,1)} %bitcast.194, bf16[768,2048]{1,0:T(8,128)(2,1)} %bitcast.159), kind=kOutput, calls=%fused_computation.141 | convolution fusion | flops 1207959552 | bytes 5898240 | tf_op jit(solution)/shard_map/dot_general | solution.py:153
  238.4 0.8 copy-done.7
  239.2 3.6 convolution_convert_fusion.1
  243.3 0.8 fusion.14.refs_1_
  244.1 29.7 %shard_map.119 = (bf16[4,96,2048]{2,1,0:T(8,128)(2,1)}, bf16[4,64,2048]{2,1,0:T(8,128)(2,1)}) custom-call(bf16[4,96,2048]{2,1,0:T(8,128)(2,1)} %bitcast.163, bf16[64,2048]{1,0:T(8,128)(2,1)} %fusion.14.refs_1_), custom_call_target="tpu_custom_call" | custom-call | bytes 64000000 | tf_op jit(solution)/shard_map/pallas_call | solution.py:103
  273.8 3.2 convolution_convert_fusion.4
  277.0 0.7 fusion.60
  277.9 1.7 fusion.2
  279.7 30.6 %shard_map.120 = (bf16[4,96,2048]{2,1,0:T(8,128)(2,1)}, bf16[4,64,2048]{2,1,0:T(8,128)(2,1)}) custom-call(bf16[4,96,2048]{2,1,0:T(8,128)(2,1)} %bitcast.145, bf16[4,64,2048]{2,1,0:T(8,128)(2,1)} %bitcast.155), custom_call_target="tpu_custom_call" | custom-call | bytes 64000000 | tf_op jit(solution)/shard_map/pallas_call | solution.py:103
  310.3 1.5 convert_reduce_fusion.1
  312.0 3.3 fusion.61
  315.4 3.6 convolution_convert_fusion
  318.9 23.9 %shard_map.121 = bf16[4,96,2048]{2,1,0:T(8,128)(2,1)} custom-call(bf16[4,96,2048]{2,1,0:T(8,128)(2,1)} %bitcast.165), custom_call_target="tpu_custom_call" | custom-call | bytes 64000000 | tf_op jit(solution)/shard_map/pallas_call | solution.py:103
  342.9 2.3 fusion.62
  345.2 1.7 fusion.3
  346.9 29.4 %shard_map.122 = bf16[4,64,2048]{2,1,0:T(8,128)(2,1)} custom-call(bf16[4,64,2048]{2,1,0:T(8,128)(2,1)} %bitcast.156), custom_call_target="tpu_custom_call" | custom-call | bytes 64000000 | tf_op jit(solution)/shard_map/pallas_call | solution.py:103
  376.3 1.4 convert_reduce_fusion
  377.8 0.8 fusion.33
  378.5 0.8 fusion.32
  (101 shorter events, 3.9 us)
Async XLA Ops:
  0.6 33.9 %copy-start.14 = (bf16[1,192,2048]{2,1,0:T(8,128)(2,1)S(1)}, bf16[1,192,2048]{2,1,0:T(8,128)(2,1)}, u32[]{:S(2)}) copy-start(bf16[1,192,2048]{2,1,0:T(8,128)(2,1)} %param.15) | copy-start | bytes 2359300
  34.6 8.7 %copy-start.26 = (f32[4,16,128]{2,1,0:T(8,128)S(1)}, f32[4,16,128]{2,1,0:T(8,128)}, u32[]{:S(2)}) copy-start(f32[4,16,128]{2,1,0:T(8,128)} %get-tuple-element.21) | copy-start | bytes 98308
  36.2 20.7 %copy-start.10 = (bf16[4,64,2048]{2,1,0:T(8,128)(2,1)S(1)}, bf16[4,64,2048]{2,1,0:T(8,128)(2,1)}, u32[]{:S(2)}) copy-start(bf16[4,64,2048]{2,1,0:T(8,128)(2,1)} %get-tuple-element.22) | copy-start | bytes 3145732
  36.2 62.4 %collective-permute-start = (bf16[576,2048]{1,0:T(8,128)(2,1)S(1)}, bf16[576,2048]{1,0:T(8,128)(2,1)}, u32[]{:S(2)}, u32[]{:S(2)}) collective-permute-start(bf16[576,2048]{1,0:T(8,128)(2,1)S(1)} %pad_maximum_fusion.1), channel_id=1, source_target_pairs={{0,1},{1,0},{2,3},{3,2},{4,5},{5,4},{6,7},{7,6},{8,9},{9,8},{10,11... | collective-permute-start | bytes 7077896 | tf_op jit(solution)/shard_map/ppermute | solution.py:24
  47.4 0.6 copy-start.18
  47.5 2.4 copy-start.19
  47.6 2.3 copy-start.20
  48.1 1.8 copy-start.21
  100.7 4.0 %copy-start.1 = (bf16[3,2,192,2048]{3,2,1,0:T(8,128)(2,1)}, bf16[3,2,192,2048]{3,2,1,0:T(8,128)(2,1)S(1)}, u32[]{:S(2)}) copy-start(bf16[3,2,192,2048]{3,2,1,0:T(8,128)(2,1)S(1)} %pad_maximum_fusion) | copy-start | bytes 14155780
  100.7 2.6 copy-start.8
  100.9 3.8 copy-start.5
  107.0 24.6 %copy-start.24 = (pred[384,256]{1,0:T(32,128)(4,1)S(1)}, pred[384,256]{1,0:T(32,128)(4,1)}, u32[]{:S(2)}) copy-start(pred[384,256]{1,0:T(32,128)(4,1)} %and.243) | copy-start | bytes 294916
  131.6 3.2 copy-start.2
  131.6 3.2 copy-start.17
  134.8 0.9 copy-start.13
  137.6 31.9 %copy-start.6 = (bf16[1,64,2048]{2,1,0:T(8,128)(2,1)S(1)}, bf16[1,64,2048]{2,1,0:T(8,128)(2,1)}, u32[]{:S(2)}) copy-start(bf16[1,64,2048]{2,1,0:T(8,128)(2,1)} %param.10) | copy-start | bytes 786436
  167.9 1.7 copy-start.27
  173.0 6.0 %copy-start.25 = (f32[1,2048]{1,0:T(1,128)S(1)}, f32[1,2048]{1,0:T(1,128)}, u32[]{:S(2)}) copy-start(f32[1,2048]{1,0:T(1,128)} %param.12) | copy-start | bytes 24580
  173.0 5.8 %collective-permute-start.1 = (bf16[64,2048]{1,0:T(8,128)(2,1)S(1)}, bf16[64,2048]{1,0:T(8,128)(2,1)S(1)}, u32[]{:S(2)}, u32[]{:S(2)}) collective-permute-start(bf16[64,2048]{1,0:T(8,128)(2,1)S(1)} %fusion.19), channel_id=1, source_target_pairs={{480,0},{0,32},{32,64},{64,96},{96,128},{128,160},{160,192},{192,2... | collective-permute-start | bytes 786440 | tf_op jit(solution)/shard_map/ppermute | solution.py:20
  176.7 26.3 %copy-start.23 = (pred[384,256]{1,0:T(32,128)(4,1)S(1)}, pred[384,256]{1,0:T(32,128)(4,1)}, u32[]{:S(2)}) copy-start(pred[384,256]{1,0:T(32,128)(4,1)} %and.258) | copy-start | bytes 294916
  203.0 3.2 copy-start.3
  234.3 3.9 %copy-start.9 = (bf16[4,64,2048]{2,1,0:T(8,128)(2,1)S(1)}, bf16[4,64,2048]{2,1,0:T(8,128)(2,1)}, u32[]{:S(2)}) copy-start(bf16[4,64,2048]{2,1,0:T(8,128)(2,1)} %get-tuple-element.31) | copy-start | bytes 3145732
  238.2 1.0 copy-start.7
  239.2 3.9 %collective-permute-start.2 = (bf16[64,2048]{1,0:T(8,128)(2,1)S(1)}, bf16[64,2048]{1,0:T(8,128)(2,1)S(1)}, u32[]{:S(2)}, u32[]{:S(2)}) collective-permute-start(bf16[64,2048]{1,0:T(8,128)(2,1)S(1)} %fusion.23), channel_id=1, source_target_pairs={{32,0},{64,32},{96,64},{128,96},{160,128},{192,160},{224,192},{256... | collective-permute-start | bytes 786440 | tf_op jit(solution)/shard_map/ppermute | solution.py:20
  242.9 31.0 %copy-start.22 = (pred[384,256]{1,0:T(32,128)(4,1)S(1)}, pred[384,256]{1,0:T(32,128)(4,1)}, u32[]{:S(2)}) copy-start(pred[384,256]{1,0:T(32,128)(4,1)} %and.253) | copy-start | bytes 294916
  273.8 3.2 copy-start.4
  273.8 3.2 copy-start.16
  277.0 0.9 copy-start.12
  310.3 1.7 copy-start.28
  318.9 23.9 %copy-start.15 = (bf16[384,256]{1,0:T(8,128)(2,1)S(1)}, bf16[384,256]{1,0:T(8,128)(2,1)}, u32[]{:S(2)}) copy-start(bf16[384,256]{1,0:T(8,128)(2,1)} %convert_element_type.384) | copy-start | bytes 589828
  342.9 2.3 copy-start
  342.9 2.3 copy-start.11

commit v4 on v3

--- a/solution.py
+++ b/solution.py
@@ -35,9 +35,57 @@
 def exchange_kernel(jobs, *refs):
     count = len(jobs)
     ins, outs = refs[:count], refs[count : 2 * count]
-    relays = refs[2 * count : 3 * count]
-    send, recv = refs[3 * count :]
+    relays, owns = refs[2 * count : 3 * count], refs[3 * count : 4 * count]
+    send, recv, local = refs[4 * count :]
     rings = {axis: neighbours(axis) for axis in dict.fromkeys(axis for axis, _ in jobs)}
+    first, later, direct, loads, stores = [], [], [], [], []
+
+    def copy(job, number, src, dst, way):
+        return pltpu.make_async_remote_copy(
+            src_ref=src,
+            dst_ref=dst,
+            send_sem=send.at[job, number],
+            recv_sem=recv.at[job, number],
+            device_id={"expert": rings[jobs[job][0]][way]},
+            device_id_type=pl.DeviceIdType.MESH,
+        )
+
+    for job, (_, kind) in enumerate(jobs):
+        src, dst, relay, own = ins[job], outs[job], relays[job], owns[job]
+        rows = dst.shape[1]
+        low, high = pl.ds(0, rows // 2), pl.ds(rows // 2, rows // 2)
+        if kind == "gather":
+            first.append(copy(job, 0, src.at[low], dst.at[1, low], 0))
+            first.append(copy(job, 1, src.at[high], dst.at[3, high], 1))
+            direct.append(copy(job, 2, src.at[high], dst.at[1, high], 0))
+            direct.append(copy(job, 3, src.at[low], dst.at[3, low], 1))
+            later.append(copy(job, 4, dst.at[1, low], dst.at[2, low], 0))
+            later.append(copy(job, 5, dst.at[3, high], dst.at[2, high], 1))
+            loads.append([(src, own)])
+        elif kind == "reduce":
+            first.append(copy(job, 0, src.at[2, low], relay.at[0], 0))
+            first.append(copy(job, 1, src.at[2, high], relay.at[1], 1))
+            direct.append(copy(job, 2, src.at[3, high], dst.at[0, high], 0))
+            direct.append(copy(job, 3, src.at[1, low], dst.at[1, low], 1))
+            later.append(copy(job, 4, relay.at[0], dst.at[0, low], 0))
+            later.append(copy(job, 5, relay.at[1], dst.at[1, high], 1))
+            loads.append([(src.at[3, low], own.at[low]), (src.at[1, high], own.at[high])])
+        else:
+            there, back = (0, 1) if kind == "swap" else (1, 0)
+            first.append(copy(job, 0, src.at[2, low], relay.at[0], 0))
+            first.append(copy(job, 1, src.at[2, high], relay.at[1], 1))
+            direct.append(copy(job, 2, src.at[1], dst.at[1], there))
+            direct.append(copy(job, 3, src.at[3], dst.at[3], back))
+            later.append(copy(job, 4, relay.at[0], dst.at[2, low], 0))
+            later.append(copy(job, 5, relay.at[1], dst.at[2, high], 1))
+            loads.append([(src.at[0], own)])
+        loads[job] = [
+            pltpu.make_async_copy(one, two, local.at[job, number])
+            for number, (one, two) in enumerate(loads[job])
+        ]
+        for load in loads[job]:
+            load.start()
+
     barrier = pltpu.get_barrier_semaphore()
     for pair in rings.values():
         for other in pair:
@@ -48,67 +96,51 @@
                 device_id_type=pl.DeviceIdType.MESH,
             )
     pl.semaphore_wait(barrier, 2 * len(rings))
-
-    def copy(job, number, src, dst, way):
-        return pltpu.make_async_remote_copy(
-            src_ref=src,
-            dst_ref=dst,
-            send_sem=send.at[job, number],
-            recv_sem=recv.at[job, number],
-            device_id={"expert": rings[jobs[job][0]][way]},
-            device_id_type=pl.DeviceIdType.MESH,
-        )
-
-    first, later, direct = [], [], []
-    for job, (_, kind) in enumerate(jobs):
-        src, dst, relay = ins[job], outs[job], relays[job]
-        rows = dst.shape[1]
-        low, high = pl.ds(0, rows // 2), pl.ds(rows // 2, rows // 2)
-        if kind == "gather":
-            first.append(copy(job, 0, src.at[low], dst.at[1, low], 0))
-            first.append(copy(job, 1, src.at[high], dst.at[3, high], 1))
-            direct.append(copy(job, 2, src.at[high], dst.at[1, high], 0))
-            direct.append(copy(job, 3, src.at[low], dst.at[3, low], 1))
-            later.append(copy(job, 4, dst.at[1, low], dst.at[2, low], 0))
-            later.append(copy(job, 5, dst.at[3, high], dst.at[2, high], 1))
-        else:
-            there, back = (0, 1) if kind == "swap" else (1, 0)
-            first.append(copy(job, 0, src.at[2, low], relay.at[0], 0))
-            first.append(copy(job, 1, src.at[2, high], relay.at[1], 1))
-            direct.append(copy(job, 2, src.at[1], dst.at[1], there))
-            direct.append(copy(job, 3, src.at[3], dst.at[3], back))
-            later.append(copy(job, 4, relay.at[0], dst.at[2, low], 0))
-            later.append(copy(job, 5, relay.at[1], dst.at[2, high], 1))
     for one in first + direct:
         one.start()
     for job, (_, kind) in enumerate(jobs):
-        outs[job][0] = ins[job][...] if kind == "gather" else ins[job][0]
-    for early, late in zip(first, later):
+        for load in loads[job]:
+            load.wait()
+        if kind != "reduce":
+            stores.append(pltpu.make_async_copy(owns[job], outs[job].at[0], local.at[job, 2]))
+            stores[-1].start()
+    for number, (early, late) in enumerate(zip(first, later)):
         early.wait_recv()
+        job, part = number // 2, number % 2
+        if jobs[job][1] == "reduce":
+            relay, rows = relays[job], owns[job].shape[0] // 2
+            mine = owns[job][pl.ds(part * rows, rows)]
+            total = relay[part].astype(jnp.float32) + mine.astype(jnp.float32)
+            relay[part] = total.astype(relay.dtype)
         late.start()
     for one in first:
         one.wait_send()
-    for one in direct + later:
+    for one in direct + later + stores:
         one.wait()
 
 
 def exchange(number, jobs, *arrays):
-    shapes, relays, sent = [], [], 0
+    shapes, relays, owns = [], [], []
     for (_, kind), array in zip(jobs, arrays):
         rows, width = array.shape[-2:]
-        shapes.append(jax.ShapeDtypeStruct((RING, rows, width), array.dtype))
+        blocks = 2 if kind == "reduce" else RING
+        shapes.append(jax.ShapeDtypeStruct((blocks, rows, width), array.dtype))
         relays.append(pltpu.VMEM((2, rows // 2, width), array.dtype))
-        sent += 4 * rows * width * 2
-    whole = pl.BlockSpec(memory_space=pltpu.VMEM)
+        owns.append(pltpu.VMEM((rows, width), array.dtype))
+    anywhere = pl.BlockSpec(memory_space=pl.ANY)
     return pl.pallas_call(
         functools.partial(exchange_kernel, jobs),
         out_shape=shapes,
-        in_specs=[whole] * len(jobs),
-        out_specs=[whole] * len(jobs),
+        in_specs=[anywhere] * len(jobs),
+        out_specs=[anywhere] * len(jobs),
         scratch_shapes=relays
-        + [pltpu.SemaphoreType.DMA((len(jobs), 6)), pltpu.SemaphoreType.DMA((len(jobs), 6))],
+        + owns
+        + [pltpu.SemaphoreType.DMA((len(jobs), 6))] * 2
+        + [pltpu.SemaphoreType.DMA((len(jobs), 3))],
         cost_estimate=pl.CostEstimate(flops=0, bytes_accessed=64_000_000, transcendentals=0),
-        compiler_params=pltpu.CompilerParams(collective_id=number, has_side_effects=True),
+        compiler_params=pltpu.CompilerParams(
+            collective_id=number, has_side_effects=True, vmem_limit_bytes=8 * 1024 * 1024
+        ),
     )(*arrays)
 
 
@@ -167,17 +199,17 @@
     return moe.astype(jnp.bfloat16).reshape(RING, -1, width)
 
 
-def finished(hidden, partial):
-    moe = jnp.sum(partial.astype(jnp.float32), axis=0)
+def finished(hidden, own, partial):
+    moe = jnp.sum(partial.astype(jnp.float32), axis=0) + own[0].astype(jnp.float32)
     return (hidden.astype(jnp.float32) + moe).astype(jnp.bfloat16)
 
 
 X_THERE = (("x", "swap"),)
 X_BACK = (("x", "back"),)
-Z_BACK = (("z", "back"),)
+Z_BACK = (("z", "reduce"),)
 START = (("z", "gather"), ("z", "gather"))
 GATHER = (("x", "back"), ("z", "gather"))
-RETURN = (("x", "swap"), ("z", "back"))
+RETURN = (("x", "swap"), ("z", "reduce"))
 
 
 def body(
@@ -221,25 +253,24 @@
         fwd_rows, rev_rows = exchange(
             3, GATHER, expert_rows(fwd_rows, *weights), normed_rows(rev, gain_row)
         )
-        rev_rows, fwd_rows = exchange(
-            4, RETURN, picked(rev_plan, rev_rows), combined(fwd_plan, fwd_rows)
-        )
-        fwd = finished(fwd, fwd_rows)
+        own = combined(fwd_plan, fwd_rows)
+        rev_rows, fwd_rows = exchange(4, RETURN, picked(rev_plan, rev_rows), own)
+        fwd = finished(fwd, own, fwd_rows)
         if tick + 1 < TICKS:
             fwd = from_behind(fwd, "pipe", 1)
             fwd_plan = plan(0, tick + 1)
             rev_rows, fwd_rows = exchange(
                 3, GATHER, expert_rows(rev_rows, *weights), normed_rows(fwd, gain_row)
             )
-            fwd_rows, rev_rows = exchange(
-                4, RETURN, picked(fwd_plan, fwd_rows), combined(rev_plan, rev_rows)
-            )
-            rev = from_behind(finished(rev, rev_rows), "pipe", -1)
+            own = combined(rev_plan, rev_rows)
+            fwd_rows, rev_rows = exchange(4, RETURN, picked(fwd_plan, fwd_rows), own)
+            rev = from_behind(finished(rev, own, rev_rows), "pipe", -1)
             rev_plan = plan(1, tick + 1)
         else:
             (rev_rows,) = exchange(6, X_BACK, expert_rows(rev_rows, *weights))
-            (rev_rows,) = exchange(5, Z_BACK, combined(rev_plan, rev_rows))
-            rev = finished(rev, rev_rows)
+            own = combined(rev_plan, rev_rows)
+            (rev_rows,) = exchange(5, Z_BACK, own)
+            rev = finished(rev, own, rev_rows)
     return (fwd[None], rev[None])
 
 

time: 381 us -> 307 us (0.81)
  the two profiles are of different devices: /device:TPU:40 before, /device:TPU:24 now
where the time goes in v4:
time: 307 us; the launch traced here: 306 us
  Pallas kernels  229 us (75%)
  other arithmetic  22 us (7%)
  matrix products  18 us (6%)
  waiting for transfers between devices  14.6 us (5%)
  local copies, waits for them, and re-layouts  14.5 us (5%)
  starting transfers between devices  7 us (2%)
    pallas_call x10, Pallas kernels, exchange(): pl.pallas_call(functools.partial(exchange_kernel, jobs), out_shape=shapes...  229 us
    convert_element_type x8, local copies, waits for them, and re-layouts, routing(): jnp.where(block, part[:, :, None, None, :], 0.0).astype(jnp.bfloat16)  9.79 us
    ppermute x2, waiting for transfers between devices, from_behind(): return lax.ppermute(block, axis, route)  7.58 us
    ppermute x1, waiting for transfers between devices, from_partner(): return lax.ppermute(block, 'expert', [(i, i ^ 1) for i in range(NX * NZ)])  7 us
    ppermute x1, starting transfers between devices, from_partner(): return lax.ppermute(block, 'expert', [(i, i ^ 1) for i in range(NX * NZ)])  6.97 us
  transfers between devices with their start and end apart: 3, of which 3 were waited for; matrix products, arithmetic and copies ran while one was open for 8% of the time, Pallas kernels for 7%

profile of v4, /device:TPU:24, one launch (start us, length us, event | category | flops | bytes accessed | tf_op | source)
XLA Modules:
  0.0 306.2 jit_solution(13280348752744340409)
XLA Ops:
  0.6 1.2 fusion.16
  1.9 1.1 fusion.20
  3.0 0.7 fusion.46
  3.7 0.7 pad_maximum_fusion.2
  4.4 1.2 fusion.22
  5.7 25.7 %shard_map.113 = (bf16[4,64,2048]{2,1,0:T(8,128)(2,1)S(1)}, f32[4,16,128]{2,1,0:T(8,128)S(1)}) custom-call(bf16[64,2048]{1,0:T(8,128)(2,1)S(1)} %get-tuple-element.69.refs_0_, f32[16,128]{1,0:T(8,128)S(1)} %pad.4.refs_1_), custom_call_target="tpu_custom_call" | custom-call | bytes 64000000 | tf_op jit(solution)/shard_map/pallas_call | solution.py:131
  31.4 2.8 pad_maximum_fusion.1
  34.2 7.0 %collective-permute-start = (bf16[576,2048]{1,0:T(8,128)(2,1)}, bf16[576,2048]{1,0:T(8,128)(2,1)}, u32[]{:S(2)}, u32[]{:S(2)}) collective-permute-start(bf16[576,2048]{1,0:T(8,128)(2,1)} %pad_maximum_fusion.1), channel_id=1, source_target_pairs={{0,1},{1,0},{2,3},{3,2},{4,5},{5,4},{6,7},{7,6},{8,9},{9,8},{10,11... | collective-permute-start | bytes 7077896 | tf_op jit(solution)/shard_map/ppermute | solution.py:24
  41.5 1.0 reduce_window_sum.23
  42.5 0.9 reduce_window_sum.27
  43.4 0.9 reduce_window_sum.32
  44.4 0.9 reduce_window_sum.22
  45.6 1.1 broadcast_and_fusion.2
  46.7 0.4 and.248
  47.1 1.0 and.253
  48.1 1.0 and.258
  49.1 1.0 and.243
  50.1 0.6 convolution_convert_fusion.7
  50.8 21.9 %shard_map.114 = bf16[4,96,2048]{2,1,0:T(8,128)(2,1)S(1)} custom-call(bf16[4,96,2048]{2,1,0:T(8,128)(2,1)S(1)} %bitcast.140), custom_call_target="tpu_custom_call" | custom-call | bytes 64000000 | tf_op jit(solution)/shard_map/pallas_call | solution.py:131
  72.8 3.2 %select_convert_fusion = (bf16[4,4,24,4,64]{4,3,2,1,0:T(4,128)(2,1)}, bf16[4,4,24,4,64]{4,3,2,1,0:T(4,128)(2,1)}, bf16[4,4,24,4,64]{4,3,2,1,0:T(4,128)(2,1)}, bf...) fusion(bf16[4,4,64]{2,1,0:T(4,128)(2,1)S(1)} %get-tuple-element, ...), kind=kLoop, calls=%fused_computation.29 | loop fusion | flops 1179648 | bytes 1687568 | tf_op jit(solution)/shard_map/convert_element_type | solution.py:170
  76.1 2.0 convert_element_type.403
  78.1 2.0 convert_element_type.399
  80.1 2.0 convert_element_type.391
  82.1 2.0 convert_element_type.393
  84.1 1.0 convert_element_type.359
  85.1 0.3 convert_element_type.361
  85.3 0.3 convert_element_type.378
  85.6 0.3 convert_element_type.380
  85.9 7.0 %collective-permute-done = bf16[576,2048]{1,0:T(8,128)(2,1)} collective-permute-done((bf16[576,2048]{1,0:T(8,128)(2,1)}, bf16[576,2048]{1,0:T(8,128)(2,1)}, u32[]{:S(2)}, u32[]{:S(2)}) %collective-permute-start) | collective-permute-done | bytes 2359328 | tf_op jit(solution)/shard_map/ppermute | solution.py:24
  92.9 2.8 pad_maximum_fusion
  95.7 0.2 slice.98
  95.9 1.4 fusion.55
  97.4 1.0 convolution_convert_fusion.3
  98.4 24.6 %shard_map.115 = (bf16[4,96,2048]{2,1,0:T(8,128)(2,1)S(1)}, bf16[4,64,2048]{2,1,0:T(8,128)(2,1)S(1)}) custom-call(bf16[4,96,2048]{2,1,0:T(8,128)(2,1)S(1)} %bitcast.154, bf16[64,2048]{1,0:T(8,128)(2,1)S(1)} %get-tuple-element.68.refs_1_), custom_call_target="tpu_custom_call" | custom-call | bytes 64000000 | tf_op jit(solution)/shard_map/pallas_call | solution.py:131
  123.0 0.6 convolution_convert_fusion.6
  123.6 0.3 copy-done.8
  123.9 0.7 fusion.56
  124.7 0.7 fusion
  125.4 19.3 %shard_map.116 = (bf16[4,96,2048]{2,1,0:T(8,128)(2,1)S(1)}, bf16[2,64,2048]{2,1,0:T(8,128)(2,1)S(1)}) custom-call(bf16[4,96,2048]{2,1,0:T(8,128)(2,1)S(1)} %bitcast.137, bf16[4,64,2048]{2,1,0:T(8,128)(2,1)S(1)} %bitcast.150), custom_call_target="tpu_custom_call" | custom-call | bytes 64000000 | tf_op jit(solution)/shard_map/pallas_call | solution.py:131
  144.9 1.4 fusion.57
  146.4 1.0 convolution_convert_fusion.2
  147.4 4.7 %collective-permute-done.1 = bf16[64,2048]{1,0:T(8,128)(2,1)S(1)} collective-permute-done((bf16[64,2048]{1,0:T(8,128)(2,1)S(1)}, bf16[64,2048]{1,0:T(8,128)(2,1)S(1)}, u32[]{:S(2)}, u32[]{:S(2)}) %collective-permute-start.1) | collective-permute-done | bytes 262176 | tf_op jit(solution)/shard_map/ppermute | solution.py:20
  152.5 24.9 %shard_map.117 = (bf16[4,96,2048]{2,1,0:T(8,128)(2,1)S(1)}, bf16[4,64,2048]{2,1,0:T(8,128)(2,1)S(1)}) custom-call(bf16[4,96,2048]{2,1,0:T(8,128)(2,1)S(1)} %bitcast.152, bf16[64,2048]{1,0:T(8,128)(2,1)S(1)} %fusion.10.refs_1_), custom_call_target="tpu_custom_call" | custom-call | bytes 64000000 | tf_op jit(solution)/shard_map/pallas_call | solution.py:131
  177.4 0.6 convolution_convert_fusion.5
  178.0 0.7 fusion.58
  178.7 0.7 fusion.1
  179.5 21.9 %shard_map.118 = (bf16[4,96,2048]{2,1,0:T(8,128)(2,1)S(1)}, bf16[2,64,2048]{2,1,0:T(8,128)(2,1)S(1)}) custom-call(bf16[4,96,2048]{2,1,0:T(8,128)(2,1)S(1)} %bitcast.138, bf16[4,64,2048]{2,1,0:T(8,128)(2,1)S(1)} %bitcast.148), custom_call_target="tpu_custom_call" | custom-call | bytes 64000000 | tf_op jit(solution)/shard_map/pallas_call | solution.py:131
  201.4 1.4 fusion.59
  203.0 1.0 convolution_convert_fusion.1
  204.1 2.8 collective-permute-done.2
  207.2 22.9 %shard_map.119 = (bf16[4,96,2048]{2,1,0:T(8,128)(2,1)S(1)}, bf16[4,64,2048]{2,1,0:T(8,128)(2,1)S(1)}) custom-call(bf16[4,96,2048]{2,1,0:T(8,128)(2,1)S(1)} %bitcast.153, bf16[64,2048]{1,0:T(8,128)(2,1)S(1)} %fusion.14.refs_1_), custom_call_target="tpu_custom_call" | custom-call | bytes 64000000 | tf_op jit(solution)/shard_map/pallas_call | solution.py:131
  230.1 0.6 convolution_convert_fusion.4
  230.7 0.3 copy-done.7
  231.0 0.7 fusion.60
  231.9 0.7 fusion.2
  232.7 24.0 %shard_map.120 = (bf16[4,96,2048]{2,1,0:T(8,128)(2,1)S(1)}, bf16[2,64,2048]{2,1,0:T(8,128)(2,1)S(1)}) custom-call(bf16[4,96,2048]{2,1,0:T(8,128)(2,1)S(1)} %bitcast.139, bf16[4,64,2048]{2,1,0:T(8,128)(2,1)S(1)} %bitcast.147), custom_call_target="tpu_custom_call" | custom-call | bytes 64000000 | tf_op jit(solution)/shard_map/pallas_call | solution.py:131
  256.7 1.4 fusion.61
  258.2 1.0 convolution_convert_fusion
  259.2 21.7 %shard_map.121 = bf16[4,96,2048]{2,1,0:T(8,128)(2,1)S(1)} custom-call(bf16[4,96,2048]{2,1,0:T(8,128)(2,1)S(1)} %bitcast.155), custom_call_target="tpu_custom_call" | custom-call | bytes 64000000 | tf_op jit(solution)/shard_map/pallas_call | solution.py:131
  281.0 0.7 fusion.62
  281.9 0.7 fusion.3
  282.6 21.9 %shard_map.122 = bf16[2,64,2048]{2,1,0:T(8,128)(2,1)S(1)} custom-call(bf16[4,64,2048]{2,1,0:T(8,128)(2,1)S(1)} %bitcast.149), custom_call_target="tpu_custom_call" | custom-call | bytes 64000000 | tf_op jit(solution)/shard_map/pallas_call | solution.py:131
  304.6 0.8 fusion.33
  305.4 0.8 fusion.32
  (77 shorter events, 2.1 us)
Async XLA Ops:
  0.6 30.7 %copy-start.4 = (bf16[1,192,2048]{2,1,0:T(8,128)(2,1)S(1)}, bf16[1,192,2048]{2,1,0:T(8,128)(2,1)}, u32[]{:S(2)}) copy-start(bf16[1,192,2048]{2,1,0:T(8,128)(2,1)} %param.15) | copy-start | bytes 2359300
  0.6 30.7 %copy-start.5 = (bf16[1,2048,192]{1,2,0:T(8,128)(2,1)S(1)}, bf16[1,2048,192]{1,2,0:T(8,128)(2,1)}, u32[]{:S(2)}) copy-start(bf16[1,2048,192]{1,2,0:T(8,128)(2,1)} %param.14) | copy-start | bytes 2359300
  34.2 58.7 %collective-permute-start = (bf16[576,2048]{1,0:T(8,128)(2,1)}, bf16[576,2048]{1,0:T(8,128)(2,1)}, u32[]{:S(2)}, u32[]{:S(2)}) collective-permute-start(bf16[576,2048]{1,0:T(8,128)(2,1)} %pad_maximum_fusion.1), channel_id=1, source_target_pairs={{0,1},{1,0},{2,3},{3,2},{4,5},{5,4},{6,7},{7,6},{8,9},{9,8},{10,11... | collective-permute-start | bytes 7077896 | tf_op jit(solution)/shard_map/ppermute | solution.py:24
  45.5 1.2 copy-start.15
  45.6 5.2 %copy-start.9 = (pred[4,4,24,64]{3,2,1,0:T(8,128)(4,1)}, pred[4,4,24,64]{3,2,1,0:T(8,128)(4,1)S(1)}, u32[]{:S(2)}) copy-start(pred[4,4,24,64]{3,2,1,0:T(8,128)(4,1)S(1)} %fusion.35) | copy-start | bytes 73732
  50.7 22.1 %copy-start.10 = (pred[4,4,24,64]{3,2,1,0:T(8,128)(4,1)S(1)}, pred[4,4,24,64]{3,2,1,0:T(8,128)(4,1)}, u32[]{:S(2)}) copy-start(pred[4,4,24,64]{3,2,1,0:T(8,128)(4,1)} %copy-done.9) | copy-start | bytes 73732
  50.7 22.1 %copy-start.16 = (pred[4,4]{1,0:T(4,128)(4,1)S(1)}, pred[4,4]{1,0:T(4,128)(4,1)}, u32[]{:S(2)}) copy-start(pred[4,4]{1,0:T(4,128)(4,1)} %copy-done.15) | copy-start | bytes 52
  98.4 24.6 %copy-start.13 = (pred[384,256]{1,0:T(32,128)(4,1)S(1)}, pred[384,256]{1,0:T(32,128)(4,1)}, u32[]{:S(2)}) copy-start(pred[384,256]{1,0:T(32,128)(4,1)} %and.243) | copy-start | bytes 294916
  123.0 0.9 copy-start.8
  125.4 19.4 %copy-start = (bf16[1,64,2048]{2,1,0:T(8,128)(2,1)S(1)}, bf16[1,64,2048]{2,1,0:T(8,128)(2,1)}, u32[]{:S(2)}) copy-start(bf16[1,64,2048]{2,1,0:T(8,128)(2,1)} %param.10) | copy-start | bytes 786436
  146.4 6.0 %copy-start.14 = (f32[1,2048]{1,0:T(1,128)S(1)}, f32[1,2048]{1,0:T(1,128)}, u32[]{:S(2)}) copy-start(f32[1,2048]{1,0:T(1,128)} %param.12) | copy-start | bytes 24580
  146.4 5.8 %collective-permute-start.1 = (bf16[64,2048]{1,0:T(8,128)(2,1)S(1)}, bf16[64,2048]{1,0:T(8,128)(2,1)S(1)}, u32[]{:S(2)}, u32[]{:S(2)}) collective-permute-start(bf16[64,2048]{1,0:T(8,128)(2,1)S(1)} %fusion.19), channel_id=1, source_target_pairs={{480,0},{0,32},{32,64},{64,96},{96,128},{128,160},{160,192},{192,2... | collective-permute-start | bytes 786440 | tf_op jit(solution)/shard_map/ppermute | solution.py:20
  147.4 30.0 %copy-start.12 = (pred[384,256]{1,0:T(32,128)(4,1)S(1)}, pred[384,256]{1,0:T(32,128)(4,1)}, u32[]{:S(2)}) copy-start(pred[384,256]{1,0:T(32,128)(4,1)} %and.258) | copy-start | bytes 294916
  201.4 1.5 copy-start.1
  203.0 3.9 %collective-permute-start.2 = (bf16[64,2048]{1,0:T(8,128)(2,1)S(1)}, bf16[64,2048]{1,0:T(8,128)(2,1)S(1)}, u32[]{:S(2)}, u32[]{:S(2)}) collective-permute-start(bf16[64,2048]{1,0:T(8,128)(2,1)S(1)} %fusion.23), channel_id=1, source_target_pairs={{32,0},{64,32},{96,64},{128,96},{160,128},{192,160},{224,192},{256... | collective-permute-start | bytes 786440 | tf_op jit(solution)/shard_map/ppermute | solution.py:20
  204.0 26.0 %copy-start.11 = (pred[384,256]{1,0:T(32,128)(4,1)S(1)}, pred[384,256]{1,0:T(32,128)(4,1)}, u32[]{:S(2)}) copy-start(pred[384,256]{1,0:T(32,128)(4,1)} %and.253) | copy-start | bytes 294916
  230.1 0.9 copy-start.7
  231.0 0.9 copy-start.3
  259.2 21.7 %copy-start.6 = (bf16[384,256]{1,0:T(8,128)(2,1)S(1)}, bf16[384,256]{1,0:T(8,128)(2,1)}, u32[]{:S(2)}) copy-start(bf16[384,256]{1,0:T(8,128)(2,1)} %convert_element_type.399) | copy-start | bytes 589828
  280.9 0.9 copy-start.2

commit v5 on v4

--- a/solution.py
+++ b/solution.py
@@ -14,12 +14,6 @@
 RING = 4
 
 
-def from_behind(block, axis, distance):
-    devices = range(lax.axis_size(axis))
-    route = [((i - distance) % len(devices), i) for i in devices]
-    return lax.ppermute(block, axis, route)
-
-
 def from_partner(block):
     return lax.ppermute(block, "expert", [(i, i ^ 1) for i in range(NX * NZ)])
 
@@ -32,23 +26,36 @@
     return x * NZ + (z + 2) % NZ, x * NZ + (z + NZ - 2) % NZ
 
 
-def exchange_kernel(jobs, *refs):
+def exchange_kernel(jobs, shift, *refs):
     count = len(jobs)
+    if shift:
+        hidden, carry = refs[count], refs[2 * count + 1]
+        refs = refs[:count] + refs[count + 1 : 2 * count + 1] + refs[2 * count + 2 :]
     ins, outs = refs[:count], refs[count : 2 * count]
     relays, owns = refs[2 * count : 3 * count], refs[3 * count : 4 * count]
     send, recv, local = refs[4 * count :]
+    me, section, sections = lax.axis_index("expert"), lax.axis_index("pipe"), lax.axis_size("pipe")
+    onward = (section + sections + shift) % sections
+    behind = (section + sections - shift) % sections
     rings = {axis: neighbours(axis) for axis in dict.fromkeys(axis for axis, _ in jobs)}
     first, later, direct, loads, stores = [], [], [], [], []
 
-    def copy(job, number, src, dst, way):
+    def remote(job, number, src, dst, device):
         return pltpu.make_async_remote_copy(
             src_ref=src,
             dst_ref=dst,
             send_sem=send.at[job, number],
             recv_sem=recv.at[job, number],
-            device_id={"expert": rings[jobs[job][0]][way]},
+            device_id=device,
             device_id_type=pl.DeviceIdType.MESH,
         )
+
+    def copy(job, number, src, dst, way):
+        return remote(job, number, src, dst, {"expert": rings[jobs[job][0]][way]})
+
+    def last(job, number, src, dst, way):
+        target = {"expert": rings[jobs[job][0]][way], "pipe": onward if shift else section}
+        return remote(job, number, src, dst, target)
 
     for job, (_, kind) in enumerate(jobs):
         src, dst, relay, own = ins[job], outs[job], relays[job], owns[job]
@@ -65,10 +72,14 @@
         elif kind == "reduce":
             first.append(copy(job, 0, src.at[2, low], relay.at[0], 0))
             first.append(copy(job, 1, src.at[2, high], relay.at[1], 1))
-            direct.append(copy(job, 2, src.at[3, high], dst.at[0, high], 0))
-            direct.append(copy(job, 3, src.at[1, low], dst.at[1, low], 1))
-            later.append(copy(job, 4, relay.at[0], dst.at[0, low], 0))
-            later.append(copy(job, 5, relay.at[1], dst.at[1, high], 1))
+            direct.append(last(job, 2, src.at[3, high], dst.at[0, high], 0))
+            direct.append(last(job, 3, src.at[1, low], dst.at[1, low], 1))
+            later.append(last(job, 4, relay.at[0], dst.at[0, low], 0))
+            later.append(last(job, 5, relay.at[1], dst.at[1, high], 1))
+            if shift:
+                ahead = {"expert": me, "pipe": onward}
+                direct.append(remote(job, 6, hidden, carry.at[0], ahead))
+                direct.append(remote(job, 7, src.at[0], carry.at[1], ahead))
             loads.append([(src.at[3, low], own.at[low]), (src.at[1, high], own.at[high])])
         else:
             there, back = (0, 1) if kind == "swap" else (1, 0)
@@ -95,7 +106,17 @@
                 device_id={"expert": other},
                 device_id_type=pl.DeviceIdType.MESH,
             )
-    pl.semaphore_wait(barrier, 2 * len(rings))
+    greeted = 2 * len(rings)
+    if shift:
+        for other in (me, *rings["z"]):
+            pl.semaphore_signal(
+                barrier,
+                inc=1,
+                device_id={"expert": other, "pipe": behind},
+                device_id_type=pl.DeviceIdType.MESH,
+            )
+        greeted += 3
+    pl.semaphore_wait(barrier, greeted)
     for one in first + direct:
         one.start()
     for job, (_, kind) in enumerate(jobs):
@@ -119,7 +140,7 @@
         one.wait()
 
 
-def exchange(number, jobs, *arrays):
+def exchange(number, jobs, *arrays, shift=0):
     shapes, relays, owns = [], [], []
     for (_, kind), array in zip(jobs, arrays):
         rows, width = array.shape[-2:]
@@ -127,15 +148,17 @@
         shapes.append(jax.ShapeDtypeStruct((blocks, rows, width), array.dtype))
         relays.append(pltpu.VMEM((2, rows // 2, width), array.dtype))
         owns.append(pltpu.VMEM((rows, width), array.dtype))
+    if shift:
+        shapes.append(jax.ShapeDtypeStruct((2,) + arrays[-1].shape, arrays[-1].dtype))
     anywhere = pl.BlockSpec(memory_space=pl.ANY)
     return pl.pallas_call(
-        functools.partial(exchange_kernel, jobs),
+        functools.partial(exchange_kernel, jobs, shift),
         out_shape=shapes,
-        in_specs=[anywhere] * len(jobs),
-        out_specs=[anywhere] * len(jobs),
+        in_specs=[anywhere] * len(arrays),
+        out_specs=[anywhere] * len(shapes),
         scratch_shapes=relays
         + owns
-        + [pltpu.SemaphoreType.DMA((len(jobs), 6))] * 2
+        + [pltpu.SemaphoreType.DMA((len(jobs), 8))] * 2
         + [pltpu.SemaphoreType.DMA((len(jobs), 3))],
         cost_estimate=pl.CostEstimate(flops=0, bytes_accessed=64_000_000, transcendentals=0),
         compiler_params=pltpu.CompilerParams(
@@ -234,13 +257,10 @@
     table = jnp.pad(table, ((0, 0), (0, 128 - tok)))
     fwd, rev = fwd_state[0], rev_state[0]
     fwd_rows, table = exchange(1, START, normed_rows(fwd, gain_row), table)
-    mine = jnp.concatenate([gate_weight[0].T, up_weight[0].T, down_weight[0]])
+    mine = (gate_weight[0].T, up_weight[0].T, down_weight[0])
     mine, fwd_rows, table = lax.optimization_barrier((mine, fwd_rows, table))
-    part = mine.shape[0] // 3
-    other = from_partner(mine)
-    both = jnp.stack([mine.reshape(3, part, -1), other.reshape(3, part, -1)], axis=1)
-    weights = lax.optimization_barrier(both.reshape(3, 2 * part, -1))
-    weights = (weights[:2].reshape(4 * part, -1), weights[2])
+    gate, up, down = [(one, from_partner(one)) for one in mine]
+    weights = lax.optimization_barrier((jnp.concatenate(gate + up), jnp.concatenate(down)))
     table = table[:, :, :tok].reshape(RING, 4, TICKS, 2, tok)
 
     def plan(stream, tick):
@@ -254,19 +274,22 @@
             3, GATHER, expert_rows(fwd_rows, *weights), normed_rows(rev, gain_row)
         )
         own = combined(fwd_plan, fwd_rows)
-        rev_rows, fwd_rows = exchange(4, RETURN, picked(rev_plan, rev_rows), own)
-        fwd = finished(fwd, own, fwd_rows)
+        rows = picked(rev_plan, rev_rows)
         if tick + 1 < TICKS:
-            fwd = from_behind(fwd, "pipe", 1)
+            rev_rows, fwd_rows, carry = exchange(7, RETURN, rows, own, fwd, shift=1)
+            fwd = finished(carry[0], carry[1:], fwd_rows)
             fwd_plan = plan(0, tick + 1)
             rev_rows, fwd_rows = exchange(
                 3, GATHER, expert_rows(rev_rows, *weights), normed_rows(fwd, gain_row)
             )
             own = combined(rev_plan, rev_rows)
-            fwd_rows, rev_rows = exchange(4, RETURN, picked(fwd_plan, fwd_rows), own)
-            rev = from_behind(finished(rev, own, rev_rows), "pipe", -1)
+            rows = picked(fwd_plan, fwd_rows)
+            fwd_rows, rev_rows, carry = exchange(8, RETURN, rows, own, rev, shift=-1)
+            rev = finished(carry[0], carry[1:], rev_rows)
             rev_plan = plan(1, tick + 1)
         else:
+            rev_rows, fwd_rows = exchange(4, RETURN, rows, own)
+            fwd = finished(fwd, own, fwd_rows)
             (rev_rows,) = exchange(6, X_BACK, expert_rows(rev_rows, *weights))
             own = combined(rev_plan, rev_rows)
             (rev_rows,) = exchange(5, Z_BACK, own)

time: 307 us -> 300 us (0.977)
  the two profiles are of different devices: /device:TPU:24 before, /device:TPU:8 now
where the time goes in v5:
time: 300 us; the launch traced here: 299 us
  Pallas kernels  230 us (77%)
  other arithmetic  20.9 us (7%)
  matrix products  17.9 us (6%)
  local copies, waits for them, and re-layouts  14.6 us (5%)
  starting transfers between devices  12.8 us (4%)
    pallas_call x10, Pallas kernels, exchange(): pl.pallas_call(functools.partial(exchange_kernel, jobs, shift), out_shape...  230 us
    ppermute x3, starting transfers between devices, from_partner(): return lax.ppermute(block, 'expert', [(i, i ^ 1) for i in range(NX * NZ)])  12.8 us
    convert_element_type x8, local copies, waits for them, and re-layouts, routing(): jnp.where(block, part[:, :, None, None, :], 0.0).astype(jnp.bfloat16)  9.75 us
  transfers between devices with their start and end apart: 3, of which 1 were waited for; matrix products, arithmetic and copies ran while one was open for 8% of the time, Pallas kernels for 7%

profile of v5, /device:TPU:8, one launch (start us, length us, event | category | flops | bytes accessed | tf_op | source)
XLA Modules:
  0.0 298.8 jit_solution(7978569373515237785)
XLA Ops:
  0.6 1.1 fusion.8
  1.7 1.1 fusion.11
  2.9 0.7 fusion.50
  3.6 0.7 pad_maximum_fusion.2
  4.3 1.2 fusion.13
  5.5 25.8 %shard_map.113 = (bf16[4,64,2048]{2,1,0:T(8,128)(2,1)S(1)}, f32[4,16,128]{2,1,0:T(8,128)S(1)}) custom-call(bf16[64,2048]{1,0:T(8,128)(2,1)S(1)} %get-tuple-element.85.refs_0_, f32[16,128]{1,0:T(8,128)S(1)} %pad.4.refs_1_), custom_call_target="tpu_custom_call" | custom-call | bytes 64000000 | tf_op jit(solution)/shard_map/pallas_call | solution.py:154
  31.3 7.0 %collective-permute-start = (bf16[192,2048]{1,0:T(8,128)(2,1)}, bf16[192,2048]{1,0:T(8,128)(2,1)}, u32[]{:S(2)}, u32[]{:S(2)}) collective-permute-start(bf16[192,2048]{1,0:T(8,128)(2,1)} %bitcast.1), channel_id=1, source_target_pairs={{0,1},{1,0},{2,3},{3,2},{4,5},{5,4},{6,7},{7,6},{8,9},{9,8},{10,11... | collective-permute-start | bytes 2359304 | tf_op jit(solution)/shard_map/ppermute | solution.py:18
  38.3 1.9 collective-permute-start.1
  40.2 3.9 %collective-permute-start.2 = (bf16[192,2048]{1,0:T(8,128)(2,1)}, bf16[192,2048]{1,0:T(8,128)(2,1)}, u32[]{:S(2)}, u32[]{:S(2)}) collective-permute-start(bf16[192,2048]{1,0:T(8,128)(2,1)} %bitcast.4), channel_id=1, source_target_pairs={{0,1},{1,0},{2,3},{3,2},{4,5},{5,4},{6,7},{7,6},{8,9},{9,8},{10,11... | collective-permute-start | bytes 2359304 | tf_op jit(solution)/shard_map/ppermute | solution.py:18
  44.6 0.6 reduce-precision_subtract_fusion
  45.2 0.9 reduce_window_sum.23
  46.1 0.9 reduce_window_sum.27
  47.1 0.9 reduce_window_sum.32
  48.0 0.9 reduce_window_sum.22
  49.0 0.6 reduce-precision_subtract_fusion.1
  49.8 1.1 broadcast_and_fusion.2
  51.0 0.4 and.248
  51.4 1.0 and.253
  52.4 1.0 and.258
  53.4 1.0 and.243
  54.4 0.6 convolution_convert_fusion.7
  55.0 21.2 %shard_map.114 = bf16[4,96,2048]{2,1,0:T(8,128)(2,1)S(1)} custom-call(bf16[4,96,2048]{2,1,0:T(8,128)(2,1)S(1)} %bitcast.168), custom_call_target="tpu_custom_call" | custom-call | bytes 64000000 | tf_op jit(solution)/shard_map/pallas_call | solution.py:154
  76.3 3.2 %select_convert_fusion = (bf16[4,4,24,4,64]{4,3,2,1,0:T(4,128)(2,1)}, bf16[4,4,24,4,64]{4,3,2,1,0:T(4,128)(2,1)}, bf16[4,4,24,4,64]{4,3,2,1,0:T(4,128)(2,1)}, bf...) fusion(bf16[4,4,64]{2,1,0:T(4,128)(2,1)S(1)} %copy-done.13, ...), kind=kLoop, calls=%fused_computation.22 | loop fusion | flops 1179648 | bytes 1687568 | tf_op jit(solution)/shard_map/convert_element_type | solution.py:193
  79.5 2.0 convert_element_type.455
  81.5 2.0 convert_element_type.451
  83.5 2.0 convert_element_type.439
  85.5 2.0 convert_element_type.441
  87.5 1.0 convert_element_type.397
  88.8 0.3 convert_element_type.423
  89.0 0.3 convert_element_type.425
  89.3 0.7 collective-permute-done.2
  90.0 1.5 pad_maximum_fusion.1
  91.5 2.0 pad_maximum_fusion
  93.5 1.4 fusion.61
  94.9 1.0 convolution_convert_fusion.3
  96.0 24.6 %shard_map.115 = (bf16[4,96,2048]{2,1,0:T(8,128)(2,1)S(1)}, bf16[4,64,2048]{2,1,0:T(8,128)(2,1)S(1)}) custom-call(bf16[4,96,2048]{2,1,0:T(8,128)(2,1)S(1)} %bitcast.186, bf16[64,2048]{1,0:T(8,128)(2,1)S(1)} %get-tuple-element.84.refs_1_), custom_call_target="tpu_custom_call" | custom-call | bytes 64000000 | tf_op jit(solution)/shard_map/pallas_call | solution.py:154
  120.7 0.6 convolution_convert_fusion.6
  121.3 0.3 copy-done.6
  121.6 0.7 fusion.62
  122.3 0.7 fusion
  123.3 22.7 %shard_map.116 = (bf16[4,96,2048]{2,1,0:T(8,128)(2,1)S(1)}, bf16[2,64,2048]{2,1,0:T(8,128)(2,1)S(1)}, bf16[2,64,2048]{2,1,0:T(8,128)(2,1)S(1)}) custom-call(bf16[4,96,2048]{2,1,0:T(8,128)(2,1)S(1)} %bitcast.169, bf16[4,64,2048]{2,1,0:T(8,128)(2,1)S(1)} %bitcast.179, bf16[64,2048]{1,0:T(8,128)(2,1)S(1)} %bitcast.181), custom_call_target="tpu_custom_call" | custom-call | bytes 64000000 | tf_op jit(solution)/shard_map/pallas_call | solution.py:154
  146.0 1.4 fusion.63
  147.7 1.0 convolution_convert_fusion.2
  148.9 24.2 %shard_map.117 = (bf16[4,96,2048]{2,1,0:T(8,128)(2,1)S(1)}, bf16[4,64,2048]{2,1,0:T(8,128)(2,1)S(1)}) custom-call(bf16[4,96,2048]{2,1,0:T(8,128)(2,1)S(1)} %bitcast.185, bf16[64,2048]{1,0:T(8,128)(2,1)S(1)} %fusion.20.refs_1_), custom_call_target="tpu_custom_call" | custom-call | bytes 64000000 | tf_op jit(solution)/shard_map/pallas_call | solution.py:154
  173.1 0.6 convolution_convert_fusion.5
  173.7 0.7 fusion.64
  174.4 0.7 fusion.1
  175.4 24.3 %shard_map.118 = (bf16[4,96,2048]{2,1,0:T(8,128)(2,1)S(1)}, bf16[2,64,2048]{2,1,0:T(8,128)(2,1)S(1)}, bf16[2,64,2048]{2,1,0:T(8,128)(2,1)S(1)}) custom-call(bf16[4,96,2048]{2,1,0:T(8,128)(2,1)S(1)} %bitcast.170, bf16[4,64,2048]{2,1,0:T(8,128)(2,1)S(1)} %bitcast.180, bf16[64,2048]{1,0:T(8,128)(2,1)S(1)} %bitcast.182), custom_call_target="tpu_custom_call" | custom-call | bytes 64000000 | tf_op jit(solution)/shard_map/pallas_call | solution.py:154
  199.7 1.4 fusion.65
  201.1 1.0 convolution_convert_fusion.1
  202.6 21.8 %shard_map.119 = (bf16[4,96,2048]{2,1,0:T(8,128)(2,1)S(1)}, bf16[4,64,2048]{2,1,0:T(8,128)(2,1)S(1)}) custom-call(bf16[4,96,2048]{2,1,0:T(8,128)(2,1)S(1)} %bitcast.184, bf16[64,2048]{1,0:T(8,128)(2,1)S(1)} %fusion.23.refs_1_), custom_call_target="tpu_custom_call" | custom-call | bytes 64000000 | tf_op jit(solution)/shard_map/pallas_call | solution.py:154
  224.5 0.6 convolution_convert_fusion.4
  225.1 0.3 copy-done.5
  225.4 0.7 fusion.66
  226.3 0.7 fusion.2
  227.1 22.8 %shard_map.120 = (bf16[4,96,2048]{2,1,0:T(8,128)(2,1)S(1)}, bf16[2,64,2048]{2,1,0:T(8,128)(2,1)S(1)}) custom-call(bf16[4,96,2048]{2,1,0:T(8,128)(2,1)S(1)} %bitcast.167, bf16[4,64,2048]{2,1,0:T(8,128)(2,1)S(1)} %bitcast.177), custom_call_target="tpu_custom_call" | custom-call | bytes 64000000 | tf_op jit(solution)/shard_map/pallas_call | solution.py:154
  250.0 0.9 fusion.29
  250.8 1.4 fusion.67
  252.3 1.0 convolution_convert_fusion
  253.3 21.5 %shard_map.121 = bf16[4,96,2048]{2,1,0:T(8,128)(2,1)S(1)} custom-call(bf16[4,96,2048]{2,1,0:T(8,128)(2,1)S(1)} %bitcast.187), custom_call_target="tpu_custom_call" | custom-call | bytes 64000000 | tf_op jit(solution)/shard_map/pallas_call | solution.py:154
  274.8 0.7 fusion.68
  275.7 0.7 fusion.3
  276.5 21.3 %shard_map.122 = bf16[2,64,2048]{2,1,0:T(8,128)(2,1)S(1)} custom-call(bf16[4,64,2048]{2,1,0:T(8,128)(2,1)S(1)} %bitcast.178), custom_call_target="tpu_custom_call" | custom-call | bytes 64000000 | tf_op jit(solution)/shard_map/pallas_call | solution.py:154
  297.9 0.9 fusion.28
  (78 shorter events, 2.7 us)
Async XLA Ops:
  31.3 60.2 %collective-permute-start = (bf16[192,2048]{1,0:T(8,128)(2,1)}, bf16[192,2048]{1,0:T(8,128)(2,1)}, u32[]{:S(2)}, u32[]{:S(2)}) collective-permute-start(bf16[192,2048]{1,0:T(8,128)(2,1)} %bitcast.1), channel_id=1, source_target_pairs={{0,1},{1,0},{2,3},{3,2},{4,5},{5,4},{6,7},{7,6},{8,9},{9,8},{10,11... | collective-permute-start | bytes 2359304 | tf_op jit(solution)/shard_map/ppermute | solution.py:18
  38.3 53.2 %collective-permute-start.1 = (bf16[192,2048]{1,0:T(8,128)(2,1)}, bf16[192,2048]{1,0:T(8,128)(2,1)}, u32[]{:S(2)}, u32[]{:S(2)}) collective-permute-start(bf16[192,2048]{1,0:T(8,128)(2,1)} %bitcast.3), channel_id=1, source_target_pairs={{0,1},{1,0},{2,3},{3,2},{4,5},{5,4},{6,7},{7,6},{8,9},{9,8},{10,11... | collective-permute-start | bytes 2359304 | tf_op jit(solution)/shard_map/ppermute | solution.py:18
  40.2 49.8 %collective-permute-start.2 = (bf16[192,2048]{1,0:T(8,128)(2,1)}, bf16[192,2048]{1,0:T(8,128)(2,1)}, u32[]{:S(2)}, u32[]{:S(2)}) collective-permute-start(bf16[192,2048]{1,0:T(8,128)(2,1)} %bitcast.4), channel_id=1, source_target_pairs={{0,1},{1,0},{2,3},{3,2},{4,5},{5,4},{6,7},{7,6},{8,9},{9,8},{10,11... | collective-permute-start | bytes 2359304 | tf_op jit(solution)/shard_map/ppermute | solution.py:18
  44.2 6.8 %copy-start.17 = (pred[4,4]{1,0:T(4,128)(4,1)}, pred[4,4]{1,0:T(4,128)(4,1)S(1)}, u32[]{:S(2)}) copy-start(pred[4,4]{1,0:T(4,128)(4,1)S(1)} %iota_compare_fusion.4) | copy-start | bytes 52
  49.8 5.1 %copy-start.7 = (pred[4,4,24,64]{3,2,1,0:T(8,128)(4,1)}, pred[4,4,24,64]{3,2,1,0:T(8,128)(4,1)S(1)}, u32[]{:S(2)}) copy-start(pred[4,4,24,64]{3,2,1,0:T(8,128)(4,1)S(1)} %fusion.39) | copy-start | bytes 73732
  55.0 21.3 %copy-start.8 = (pred[4,4,24,64]{3,2,1,0:T(8,128)(4,1)S(1)}, pred[4,4,24,64]{3,2,1,0:T(8,128)(4,1)}, u32[]{:S(2)}) copy-start(pred[4,4,24,64]{3,2,1,0:T(8,128)(4,1)} %copy-done.7) | copy-start | bytes 73732
  55.0 21.3 %copy-start.13 = (bf16[4,4,64]{2,1,0:T(4,128)(2,1)S(1)}, bf16[4,4,64]{2,1,0:T(4,128)(2,1)}, u32[]{:S(2)}) copy-start(bf16[4,4,64]{2,1,0:T(4,128)(2,1)} %get-tuple-element.76) | copy-start | bytes 6148
  55.0 21.3 %copy-start.14 = (bf16[4,4,64]{2,1,0:T(4,128)(2,1)S(1)}, bf16[4,4,64]{2,1,0:T(4,128)(2,1)}, u32[]{:S(2)}) copy-start(bf16[4,4,64]{2,1,0:T(4,128)(2,1)} %get-tuple-element.77) | copy-start | bytes 6148
  55.0 21.3 %copy-start.15 = (bf16[4,4,64]{2,1,0:T(4,128)(2,1)S(1)}, bf16[4,4,64]{2,1,0:T(4,128)(2,1)}, u32[]{:S(2)}) copy-start(bf16[4,4,64]{2,1,0:T(4,128)(2,1)} %get-tuple-element.78) | copy-start | bytes 6148
  55.0 21.3 %copy-start.16 = (bf16[4,4,64]{2,1,0:T(4,128)(2,1)S(1)}, bf16[4,4,64]{2,1,0:T(4,128)(2,1)}, u32[]{:S(2)}) copy-start(bf16[4,4,64]{2,1,0:T(4,128)(2,1)} %get-tuple-element.79) | copy-start | bytes 6148
  55.0 21.3 %copy-start.18 = (pred[4,4]{1,0:T(4,128)(4,1)S(1)}, pred[4,4]{1,0:T(4,128)(4,1)}, u32[]{:S(2)}) copy-start(pred[4,4]{1,0:T(4,128)(4,1)} %copy-done.17) | copy-start | bytes 52
  96.0 24.7 %copy-start.11 = (pred[384,256]{1,0:T(32,128)(4,1)S(1)}, pred[384,256]{1,0:T(32,128)(4,1)}, u32[]{:S(2)}) copy-start(pred[384,256]{1,0:T(32,128)(4,1)} %and.243) | copy-start | bytes 294916
  120.6 0.9 copy-start.6
  122.3 1.0 copy-start
  147.7 1.0 copy-start.12
  148.7 24.4 %copy-start.10 = (pred[384,256]{1,0:T(32,128)(4,1)S(1)}, pred[384,256]{1,0:T(32,128)(4,1)}, u32[]{:S(2)}) copy-start(pred[384,256]{1,0:T(32,128)(4,1)} %and.258) | copy-start | bytes 294916
  174.4 1.0 copy-start.1
  202.2 22.2 %copy-start.9 = (pred[384,256]{1,0:T(32,128)(4,1)S(1)}, pred[384,256]{1,0:T(32,128)(4,1)}, u32[]{:S(2)}) copy-start(pred[384,256]{1,0:T(32,128)(4,1)} %and.253) | copy-start | bytes 294916
  224.5 0.9 copy-start.5
  225.4 0.9 copy-start.3
  253.3 21.5 %copy-start.4 = (bf16[384,256]{1,0:T(8,128)(2,1)S(1)}, bf16[384,256]{1,0:T(8,128)(2,1)}, u32[]{:S(2)}) copy-start(bf16[384,256]{1,0:T(8,128)(2,1)} %convert_element_type.451) | copy-start | bytes 589828
  274.8 0.9 copy-start.2

commit v6 on v5

--- a/solution.py
+++ b/solution.py
@@ -181,17 +181,18 @@
     chosen = jnp.any(match, axis=2)
     count = chosen.astype(jnp.int32)
     rank = jnp.cumsum(count, axis=-1) - count
-    slot = jnp.arange(CAP, dtype=jnp.int32)
-    hot = chosen[:, :, None, :] & (rank[:, :, None, :] == slot[None, None, :, None])
-    same = jnp.eye(RING, dtype=jnp.bool_)
-    block = hot[:, :, :, None, :] & same[None, :, None, :, None]
-    pick = block.astype(jnp.bfloat16).reshape(NX * RING * CAP, RING * tok)
+    lanes = RING * tok
+    rank = jnp.where(chosen, rank, -1).reshape(NX, 1, lanes)
+    row = lax.broadcasted_iota(jnp.int32, (RING * CAP, lanes), 0)
+    lane = lax.broadcasted_iota(jnp.int32, (RING * CAP, lanes), 1)
+    block = (rank == (row % CAP)[None]) & (row // CAP == lane // tok)[None]
+    pick = block.astype(jnp.bfloat16).reshape(-1, lanes)
+    weight = weight.reshape(NX, 1, lanes)
     high = lax.reduce_precision(weight, 8, 7)
-    low = weight - high
     parts = []
-    for part in (high, low):
-        spread = jnp.where(block, part[:, :, None, None, :], 0.0).astype(jnp.bfloat16)
-        parts.append(spread.reshape(NX * RING * CAP, RING * tok))
+    for part in (high, weight - high):
+        spread = jnp.where(block, part, 0.0).astype(jnp.bfloat16)
+        parts.append(spread.reshape(-1, lanes))
     return pick, parts
 
 
@@ -258,7 +259,7 @@
     fwd, rev = fwd_state[0], rev_state[0]
     fwd_rows, table = exchange(1, START, normed_rows(fwd, gain_row), table)
     mine = (gate_weight[0].T, up_weight[0].T, down_weight[0])
-    mine, fwd_rows, table = lax.optimization_barrier((mine, fwd_rows, table))
+    mine, rev, fwd_rows, table = lax.optimization_barrier((mine, rev, fwd_rows, table))
     gate, up, down = [(one, from_partner(one)) for one in mine]
     weights = lax.optimization_barrier((jnp.concatenate(gate + up), jnp.concatenate(down)))
     table = table[:, :, :tok].reshape(RING, 4, TICKS, 2, tok)

time: 300 us -> 296 us (0.987)
  waiting for transfers between devices: 0.68 us -> 17.5 us
  local copies, waits for them, and re-layouts: 14.6 us -> 1.51 us
  other arithmetic: 20.9 us -> 11.9 us
    ppermute x3, waiting for transfers between devices: 0.68 us -> 17.5 us  [from_partner(): return lax.ppermute(block, 'expert', [(i, i ^ 1) for i in range(NX * NZ)])]
    convert_element_type x8 -> x0, local copies, waits for them, and re-layouts: 9.75 us -> none  [routing(): jnp.where(block, part[:, :, None, None, :], 0.0).astype(jnp.bfloat16)]
    and x4 -> x0, local copies, waits for them, and re-layouts: 3.35 us -> none  [routing(): block = hot[:, :, :, None, :] & same[None, :, None, :, None]]
    convert_element_type x1 -> x0, other arithmetic: 3.2 us -> none  [routing(): jnp.where(block, part[:, :, None, None, :], 0.0).astype(jnp.bfloat16)]
  transfers between devices with their start and end apart: 3 -> 3, of which waited for: 1 -> 1; matrix products, arithmetic and copies ran while one was open for 8% -> 2% of each run, Pallas kernels for 7% -> 7%
where the time goes in v6:
time: 296 us; the launch traced here: 295 us
  Pallas kernels  232 us (78%)
  matrix products  18 us (6%)
  waiting for transfers between devices  17.5 us (6%)
  starting transfers between devices  12.8 us (4%)
  other arithmetic  11.9 us (4%)
    pallas_call x10, Pallas kernels, exchange(): pl.pallas_call(functools.partial(exchange_kernel, jobs, shift), out_shape...  232 us
    ppermute x3, waiting for transfers between devices, from_partner(): return lax.ppermute(block, 'expert', [(i, i ^ 1) for i in range(NX * NZ)])  17.5 us
    ppermute x3, starting transfers between devices, from_partner(): return lax.ppermute(block, 'expert', [(i, i ^ 1) for i in range(NX * NZ)])  12.8 us
  transfers between devices with their start and end apart: 3, of which 1 were waited for; matrix products, arithmetic and copies ran while one was open for 2% of the time, Pallas kernels for 7%

profile of v6, /device:TPU:8, one launch (start us, length us, event | category | flops | bytes accessed | tf_op | source)
XLA Modules:
  0.0 295.1 jit_solution(18310218181430343492)
XLA Ops:
  0.6 1.1 fusion.12
  1.7 1.1 fusion.14.refs_0_
  2.9 0.7 fusion.66
  3.6 0.7 pad_maximum_fusion.2
  4.3 25.8 %shard_map.113 = (bf16[4,64,2048]{2,1,0:T(8,128)(2,1)S(1)}, f32[4,16,128]{2,1,0:T(8,128)S(1)}) custom-call(bf16[64,2048]{1,0:T(8,128)(2,1)S(1)} %fusion.14.refs_0_, f32[16,128]{1,0:T(8,128)S(1)} %pad.4.refs_1_), custom_call_target="tpu_custom_call" | custom-call | bytes 64000000 | tf_op jit(solution)/shard_map/pallas_call | solution.py:154
  30.0 7.0 %collective-permute-start = (bf16[192,2048]{1,0:T(8,128)(2,1)}, bf16[192,2048]{1,0:T(8,128)(2,1)S(1)}, u32[]{:S(2)}, u32[]{:S(2)}) collective-permute-start(bf16[192,2048]{1,0:T(8,128)(2,1)} %bitcast.206), channel_id=1, source_target_pairs={{0,1},{1,0},{2,3},{3,2},{4,5},{5,4},{6,7},{7,6},{8,9},{9,8},{10,11... | collective-permute-start | bytes 2359304 | tf_op jit(solution)/shard_map/ppermute | solution.py:18
  37.0 1.9 collective-permute-start.1
  39.0 3.9 %collective-permute-start.2 = (bf16[192,2048]{1,0:T(8,128)(2,1)}, bf16[192,2048]{1,0:T(8,128)(2,1)S(1)}, u32[]{:S(2)}, u32[]{:S(2)}) collective-permute-start(bf16[192,2048]{1,0:T(8,128)(2,1)} %bitcast.208), channel_id=1, source_target_pairs={{0,1},{1,0},{2,3},{3,2},{4,5},{5,4},{6,7},{7,6},{8,9},{9,8},{10,11... | collective-permute-start | bytes 2359304 | tf_op jit(solution)/shard_map/ppermute | solution.py:18
  43.0 0.1 compare_reduce_fusion.2
  43.6 1.0 reduce_window_sum.26
  44.5 0.1 reduce_window_sum.30
  44.6 0.9 reduce_window_sum.43
  45.6 0.1 reduce_window_sum.44
  45.6 0.9 reduce_window_sum.41
  46.6 0.1 reduce_window_sum.42
  46.7 0.9 reduce_window_sum.31
  47.6 0.1 reduce_window_sum.40
  47.7 0.1 fusion.60
  47.8 0.1 reshape.529
  48.2 0.1 broadcast_select_fusion
  48.4 0.1 select_compare_fusion
  48.5 0.3 compare_and_fusion.2
  48.8 0.6 convolution_convert_fusion.7
  49.4 0.2 fusion.15
  49.6 21.4 %shard_map.114 = bf16[4,96,2048]{2,1,0:T(8,128)(2,1)S(1)} custom-call(bf16[4,96,2048]{2,1,0:T(8,128)(2,1)S(1)} %bitcast.175), custom_call_target="tpu_custom_call" | custom-call | bytes 64000000 | tf_op jit(solution)/shard_map/pallas_call | solution.py:154
  71.0 0.1 fusion.17.refs_1_
  71.2 17.5 %collective-permute-done.2 = bf16[192,2048]{1,0:T(8,128)(2,1)S(1)} collective-permute-done((bf16[192,2048]{1,0:T(8,128)(2,1)}, bf16[192,2048]{1,0:T(8,128)(2,1)S(1)}, u32[]{:S(2)}, u32[]{:S(2)}) %collective-permute-start.2) | collective-permute-done | bytes 786464 | tf_op jit(solution)/shard_map/ppermute | solution.py:18
  88.6 0.2 pad_maximum_fusion.1
  88.8 0.4 pad_maximum_fusion
  89.3 1.4 fusion.89
  90.7 1.0 convolution_convert_fusion.3
  91.7 24.5 %shard_map.115 = (bf16[4,96,2048]{2,1,0:T(8,128)(2,1)S(1)}, bf16[4,64,2048]{2,1,0:T(8,128)(2,1)S(1)}) custom-call(bf16[4,96,2048]{2,1,0:T(8,128)(2,1)S(1)} %bitcast.190, bf16[64,2048]{1,0:T(8,128)(2,1)S(1)} %fusion.17.refs_1_), custom_call_target="tpu_custom_call" | custom-call | bytes 64000000 | tf_op jit(solution)/shard_map/pallas_call | solution.py:154
  116.3 0.7 convolution_bitcast_fusion.6
  117.0 0.7 fusion.7
  117.8 0.6 convolution_convert_fusion.6
  118.4 0.4 copy-done
  118.7 22.6 %shard_map.116 = (bf16[4,96,2048]{2,1,0:T(8,128)(2,1)S(1)}, bf16[2,64,2048]{2,1,0:T(8,128)(2,1)S(1)}, bf16[2,64,2048]{2,1,0:T(8,128)(2,1)S(1)}) custom-call(bf16[4,96,2048]{2,1,0:T(8,128)(2,1)S(1)} %bitcast.177, bf16[4,64,2048]{2,1,0:T(8,128)(2,1)S(1)} %bitcast.181, bf16[64,2048]{1,0:T(8,128)(2,1)S(1)} %bitcast.183), custom_call_target="tpu_custom_call" | custom-call | bytes 64000000 | tf_op jit(solution)/shard_map/pallas_call | solution.py:154
  141.3 0.1 convert_reduce_fusion.3
  141.4 0.2 fusion.22
  141.7 1.4 fusion.90
  143.1 1.0 convolution_convert_fusion.2
  144.1 0.1 fusion.24.refs_1_
  144.3 24.1 %shard_map.117 = (bf16[4,96,2048]{2,1,0:T(8,128)(2,1)S(1)}, bf16[4,64,2048]{2,1,0:T(8,128)(2,1)S(1)}) custom-call(bf16[4,96,2048]{2,1,0:T(8,128)(2,1)S(1)} %bitcast.188, bf16[64,2048]{1,0:T(8,128)(2,1)S(1)} %fusion.24.refs_1_), custom_call_target="tpu_custom_call" | custom-call | bytes 64000000 | tf_op jit(solution)/shard_map/pallas_call | solution.py:154
  168.3 0.7 convolution_bitcast_fusion.4
  169.1 0.7 fusion.6
  169.8 0.6 convolution_convert_fusion.5
  170.4 24.7 %shard_map.118 = (bf16[4,96,2048]{2,1,0:T(8,128)(2,1)S(1)}, bf16[2,64,2048]{2,1,0:T(8,128)(2,1)S(1)}, bf16[2,64,2048]{2,1,0:T(8,128)(2,1)S(1)}) custom-call(bf16[4,96,2048]{2,1,0:T(8,128)(2,1)S(1)} %bitcast.178, bf16[4,64,2048]{2,1,0:T(8,128)(2,1)S(1)} %bitcast.182, bf16[64,2048]{1,0:T(8,128)(2,1)S(1)} %bitcast.186), custom_call_target="tpu_custom_call" | custom-call | bytes 64000000 | tf_op jit(solution)/shard_map/pallas_call | solution.py:154
  195.2 0.2 fusion.25
  195.4 1.4 fusion.91
  196.8 1.0 convolution_convert_fusion.1
  197.9 0.1 fusion.27.refs_1_
  198.0 21.8 %shard_map.119 = (bf16[4,96,2048]{2,1,0:T(8,128)(2,1)S(1)}, bf16[4,64,2048]{2,1,0:T(8,128)(2,1)S(1)}) custom-call(bf16[4,96,2048]{2,1,0:T(8,128)(2,1)S(1)} %bitcast.189, bf16[64,2048]{1,0:T(8,128)(2,1)S(1)} %fusion.27.refs_1_), custom_call_target="tpu_custom_call" | custom-call | bytes 64000000 | tf_op jit(solution)/shard_map/pallas_call | solution.py:154
  219.8 0.7 convolution_bitcast_fusion.2
  220.5 0.7 fusion.5
  221.3 0.6 convolution_convert_fusion.4
  221.9 22.1 %shard_map.120 = (bf16[4,96,2048]{2,1,0:T(8,128)(2,1)S(1)}, bf16[2,64,2048]{2,1,0:T(8,128)(2,1)S(1)}) custom-call(bf16[4,96,2048]{2,1,0:T(8,128)(2,1)S(1)} %bitcast.176, bf16[4,64,2048]{2,1,0:T(8,128)(2,1)S(1)} %bitcast.179), custom_call_target="tpu_custom_call" | custom-call | bytes 64000000 | tf_op jit(solution)/shard_map/pallas_call | solution.py:154
  244.0 1.4 fusion.92
  245.5 1.0 convolution_convert_fusion
  246.5 21.4 %shard_map.121 = bf16[4,96,2048]{2,1,0:T(8,128)(2,1)S(1)} custom-call(bf16[4,96,2048]{2,1,0:T(8,128)(2,1)S(1)} %bitcast.191), custom_call_target="tpu_custom_call" | custom-call | bytes 64000000 | tf_op jit(solution)/shard_map/pallas_call | solution.py:154
  267.9 0.7 convolution_bitcast_fusion
  268.6 0.7 fusion.4
  269.3 23.8 %shard_map.122 = bf16[2,64,2048]{2,1,0:T(8,128)(2,1)S(1)} custom-call(bf16[4,64,2048]{2,1,0:T(8,128)(2,1)S(1)} %bitcast.180), custom_call_target="tpu_custom_call" | custom-call | bytes 64000000 | tf_op jit(solution)/shard_map/pallas_call | solution.py:154
  293.3 0.9 fusion.32
  294.2 0.9 fusion.33
  (56 shorter events, 1.2 us)
Async XLA Ops:
  30.0 58.8 %collective-permute-start = (bf16[192,2048]{1,0:T(8,128)(2,1)}, bf16[192,2048]{1,0:T(8,128)(2,1)S(1)}, u32[]{:S(2)}, u32[]{:S(2)}) collective-permute-start(bf16[192,2048]{1,0:T(8,128)(2,1)} %bitcast.206), channel_id=1, source_target_pairs={{0,1},{1,0},{2,3},{3,2},{4,5},{5,4},{6,7},{7,6},{8,9},{9,8},{10,11... | collective-permute-start | bytes 2359304 | tf_op jit(solution)/shard_map/ppermute | solution.py:18
  37.0 51.8 %collective-permute-start.1 = (bf16[192,2048]{1,0:T(8,128)(2,1)}, bf16[192,2048]{1,0:T(8,128)(2,1)S(1)}, u32[]{:S(2)}, u32[]{:S(2)}) collective-permute-start(bf16[192,2048]{1,0:T(8,128)(2,1)} %bitcast.204), channel_id=1, source_target_pairs={{0,1},{1,0},{2,3},{3,2},{4,5},{5,4},{6,7},{7,6},{8,9},{9,8},{10,11... | collective-permute-start | bytes 2359304 | tf_op jit(solution)/shard_map/ppermute | solution.py:18
  39.0 49.7 %collective-permute-start.2 = (bf16[192,2048]{1,0:T(8,128)(2,1)}, bf16[192,2048]{1,0:T(8,128)(2,1)S(1)}, u32[]{:S(2)}, u32[]{:S(2)}) collective-permute-start(bf16[192,2048]{1,0:T(8,128)(2,1)} %bitcast.208), channel_id=1, source_target_pairs={{0,1},{1,0},{2,3},{3,2},{4,5},{5,4},{6,7},{7,6},{8,9},{9,8},{10,11... | collective-permute-start | bytes 2359304 | tf_op jit(solution)/shard_map/ppermute | solution.py:18
  48.5 1.0 copy-start.1
  49.6 21.4 %copy-start.5 = (f32[1,2048]{1,0:T(1,128)S(1)}, f32[1,2048]{1,0:T(1,128)}, u32[]{:S(2)}) copy-start(f32[1,2048]{1,0:T(1,128)} %param.12) | copy-start | bytes 24580
  49.6 39.0 %copy-start.4 = (bf16[1,192,2048]{2,1,0:T(8,128)(2,1)S(1)}, bf16[1,192,2048]{2,1,0:T(8,128)(2,1)}, u32[]{:S(2)}) copy-start(bf16[1,192,2048]{2,1,0:T(8,128)(2,1)} %param.15) | copy-start | bytes 2359300
  71.1 17.7 %copy-start.2 = (bf16[1,2048,192]{1,2,0:T(8,128)(2,1)S(1)}, bf16[1,2048,192]{1,2,0:T(8,128)(2,1)}, u32[]{:S(2)}) copy-start(bf16[1,2048,192]{1,2,0:T(8,128)(2,1)} %param.14) | copy-start | bytes 2359300
  71.1 17.7 %copy-start.3 = (bf16[1,2048,192]{1,2,0:T(8,128)(2,1)S(1)}, bf16[1,2048,192]{1,2,0:T(8,128)(2,1)}, u32[]{:S(2)}) copy-start(bf16[1,2048,192]{1,2,0:T(8,128)(2,1)} %param.13) | copy-start | bytes 2359300
  117.8 1.0 copy-start
